TPU v7x, 32 devices: a whole 2x2x4 slice. The times are simulated.
32 devices in a mesh: dp: 8 (over z, y), tensor: 4 (over x, core).
Axes of the slice: x: 2, y: 2, z: 4, core: 2. Of those that a mesh axis runs over, the one named last changes fastest.
Arguments:
- tokens: bfloat16 [8192, 1152], P(('dp', 'tensor')), may hold values from -6 to 6
- w_query: bfloat16 [1152, 1152], P(None, 'tensor'), may hold values from -0.1875 to 0.1875
- w_key: bfloat16 [1152, 1152], P(None, 'tensor'), may hold values from -0.1875 to 0.1875
- w_value: bfloat16 [1152, 1152], P(None, 'tensor'), may hold values from -0.1875 to 0.1875
- w_out: bfloat16 [1152, 1152], P('tensor'), may hold values from -1.5 to 1.5
- w_gate: bfloat16 [1152, 3072], P(None, 'tensor'), may hold values from -0.1875 to 0.1875
- w_up: bfloat16 [1152, 3072], P(None, 'tensor'), may hold values from -0.1875 to 0.1875
- w_down: bfloat16 [3072, 1152], P('tensor'), may hold values from -0.109375 to 0.109375
- w_mod: bfloat16 [1152, 6912], P('tensor'), may hold values from -0.1875 to 0.1875
- b_mod: float32 [6912], P('tensor'), may hold values from -3 to 3
- class_table: bfloat16 [1000, 1152], P(None, 'tensor'), may hold values from -6 to 6
- q_gain: float32 [72], replicated, may hold values from 0.8 to 1.8
- k_gain: float32 [72], replicated, may hold values from 0.8 to 1.8
- slot_item: int32 [8, 4], P('dp'), may hold values from -1 to 3, as said below
- labels: int32 [8, 4], P('dp'), may hold values from 0 to 999
- tsteps: int32 [8, 4], P('dp'), may hold values from 0 to 999
- cotangent: bfloat16 [8192, 1152], P(('dp', 'tensor')), may hold values from -6 to 6
Outputs:
- output: bfloat16 [8192, 1152], P(('dp', 'tensor'))
- grad_tokens: bfloat16 [8192, 1152], P(('dp', 'tensor'))
- grad_w_query: float32 [1152, 1152], P(None, 'tensor')
- grad_w_key: float32 [1152, 1152], P(None, 'tensor')
- grad_w_value: float32 [1152, 1152], P(None, 'tensor')
- grad_w_out: float32 [1152, 1152], P('tensor')
- grad_w_gate: float32 [1152, 3072], P(None, 'tensor')
- grad_w_up: float32 [1152, 3072], P(None, 'tensor')
- grad_w_down: float32 [3072, 1152], P('tensor')
- grad_w_mod: float32 [1152, 6912], P('tensor')
- grad_b_mod: float32 [6912], P('tensor')
- grad_class_table: float32 [1000, 1152], P(None, 'tensor')
- grad_q_gain: float32 [72], replicated
- grad_k_gain: float32 [72], replicated
Inputs may be any that keep to these rules, and one draw needn't show every extreme that they name: `slot_item`: on each dp index, slot s covers that index's rows s*256 to (s+1)*256 - 1 and holds the number of the item that fills it, or -1 for padding. Items are numbered 0, 1, 2 and so on in slot order; an item fills either one slot or all four slots of one aligned group of four slots.
All inputs are finite; a program needn't handle non-finite values.
Results may differ from a plain program's by a relative error of at most 0.025.
Values may be sent and summed in bfloat16 or wider, within the bound.
No kernel may reach another device: no remote copies, remote signals or barrier semaphores. Data moves between devices by JAX's collectives and lax.ppermute only.
A program may use at most 192 MiB of HBM per device.

v0:
```python
import math

import jax
import jax.numpy as jnp
from jax import lax
from jax.sharding import PartitionSpec as P

D = 1152
HEAD_DIM = 72
SIDE = 16
SLOT_TOK = 256


EPSILON = 1e-06
MASKED = -1000000000.0
CONTRACT_ROWS = (((0,), (0,)), ((), ()))
CONTRACT_COLS = (((1,), (1,)), ((), ()))


def sinusoid(step_ids, first_col, col_count):
    half_width = D // 2
    feature = first_col + jnp.arange(col_count, dtype=jnp.int32)
    freq_index = (feature % half_width).astype(jnp.float32)
    rates = jnp.exp(-math.log(10000.0) * freq_index / half_width)
    angles = step_ids.astype(jnp.float32)[:, None] * rates[None, :]
    return jnp.where(feature[None, :] < half_width, jnp.cos(angles), jnp.sin(angles))


def grid_positions(slot_ids):
    slot_count = slot_ids.shape[0]
    slot_order = jnp.arange(slot_count, dtype=jnp.int32)
    same_item = (slot_ids[:, None] == slot_ids[None, :]) & (slot_ids[:, None] >= 0)
    members = jnp.sum(same_item.astype(jnp.int32), axis=1)
    first_slot = jnp.min(jnp.where(same_item, slot_order[None, :], slot_count), axis=1)
    first_slot = jnp.where(members > 0, first_slot, slot_order)
    side_len = jnp.where(members > 1, 2 * SIDE, SIDE)
    within = jnp.arange(SLOT_TOK, dtype=jnp.int32)
    place_in = (slot_order - first_slot)[:, None] * SLOT_TOK + within[None, :]
    return ((place_in // side_len[:, None]).reshape(-1), (place_in % side_len[:, None]).reshape(-1))


def turn_half(values, grid_index):
    half_len = values.shape[-1] // 2
    rates = jnp.exp(-math.log(10000.0) * jnp.arange(half_len, dtype=jnp.float32) / half_len)
    angles = grid_index.astype(jnp.float32)[:, None] * rates[None, :]
    cosine = jnp.cos(angles)[:, None, :]
    sine_v = jnp.sin(angles)[:, None, :]
    front = values[..., :half_len]
    back_half = values[..., half_len:]
    return jnp.concatenate(
        [front * cosine - back_half * sine_v, back_half * cosine + front * sine_v], axis=-1
    )


def head_rotary(linear, head_gain, grid_row, grid_col):
    per_head = linear.reshape(linear.shape[0], -1, HEAD_DIM)
    normed = (
        per_head
        * lax.rsqrt(jnp.mean(per_head * per_head, axis=-1, keepdims=True) + EPSILON)
        * head_gain
    )
    half_dim = HEAD_DIM // 2
    return jnp.concatenate(
        [turn_half(normed[..., :half_dim], grid_row), turn_half(normed[..., half_dim:], grid_col)],
        axis=-1,
    )


def modulated_norm(values, shift_by, scale_by):
    normed = values * lax.rsqrt(jnp.mean(values * values, axis=-1, keepdims=True) + EPSILON)
    return normed * (1.0 + scale_by[:, None, :]) + shift_by[:, None, :]


def masked_scores(query_blk, key_blk, item_of):
    raw_scores = jnp.einsum(
        "qhd,khd->hqk", query_blk, key_blk, preferred_element_type=jnp.float32
    ) * (1.0 / math.sqrt(HEAD_DIM))
    allowed = item_of[:, None] == item_of[None, :]
    return jnp.where(allowed[None], raw_scores, MASKED)


def forward_group(group_args):
    query_blk, key_blk, value_blk, item_of = group_args
    scores = masked_scores(query_blk, key_blk, item_of)
    row_max = jnp.max(scores, axis=-1, keepdims=True)
    weights_exp = jnp.exp(scores - row_max)
    row_total = jnp.sum(weights_exp, axis=-1, keepdims=True)
    probs_low = (weights_exp / row_total).astype(jnp.bfloat16)
    mixed_blk = jnp.einsum("hqk,khd->qhd", probs_low, value_blk, preferred_element_type=jnp.float32)
    return (mixed_blk, (row_max + jnp.log(row_total))[..., 0])


def backward_group(group_args):
    query_blk, key_blk, value_blk, grad_blk, log_total, item_of = group_args
    scores = masked_scores(query_blk, key_blk, item_of)
    probs = jnp.exp(scores - log_total[..., None])
    grad_value = jnp.einsum(
        "hqk,qhd->khd", probs.astype(jnp.bfloat16), grad_blk, preferred_element_type=jnp.float32
    )
    grad_probs = jnp.einsum("qhd,khd->hqk", grad_blk, value_blk, preferred_element_type=jnp.float32)
    row_dot = jnp.sum(probs * grad_probs, axis=-1, keepdims=True)
    grad_scores = (probs * (grad_probs - row_dot)).astype(jnp.bfloat16)
    inv_root = 1.0 / math.sqrt(HEAD_DIM)
    grad_query = (
        jnp.einsum("hqk,khd->qhd", grad_scores, key_blk, preferred_element_type=jnp.float32)
        * inv_root
    )
    grad_key = (
        jnp.einsum("hqk,qhd->khd", grad_scores, query_blk, preferred_element_type=jnp.float32)
        * inv_root
    )
    return (grad_query, grad_key, grad_value)


def fold_rows(weight, piece_rows):
    partial_value = jnp.dot(piece_rows, weight, preferred_element_type=jnp.float32)
    return (piece_rows, partial_value)


def fold_back(kept, weight, piece_rows):
    grad_weight = lax.dot_general(
        kept, piece_rows, CONTRACT_ROWS, preferred_element_type=jnp.float32
    )
    partial_value = lax.dot_general(
        piece_rows, weight, CONTRACT_COLS, preferred_element_type=jnp.float32
    )
    return (partial_value, grad_weight)


def rows_times(source, weight, transpose_w):
    if transpose_w:
        return lax.dot_general(source, weight, CONTRACT_COLS, preferred_element_type=jnp.float32)
    return jnp.dot(source, weight, preferred_element_type=jnp.float32)


def local(
    tokens,
    w_query,
    w_key,
    w_value,
    w_out,
    w_gate,
    w_up,
    w_down,
    w_mod,
    b_mod,
    class_table,
    q_gain,
    k_gain,
    slot_item,
    labels,
    tsteps,
    cotangent,
):
    tensor_count = lax.axis_size("tensor")
    tensor_place = lax.axis_index("tensor")
    slot_ids = slot_item[0]
    slot_count = slot_ids.shape[0]
    group_count = slot_count // 4
    group_tok = 4 * SLOT_TOK
    my_slots = slot_count // tensor_count
    local_rows = tokens.shape[0]
    model_width = tokens.shape[1]
    all_rows = local_rows * tensor_count
    head_cols = w_query.shape[1]
    local_heads = head_cols // HEAD_DIM
    bias_len = b_mod.shape[0]
    item_ids = jnp.arange(labels.shape[1], dtype=jnp.int32)
    class_ids = jnp.arange(class_table.shape[0], dtype=jnp.int32)
    label_hot = (labels[0][:, None] == class_ids[None, :]).astype(jnp.float32)
    embedded = jnp.dot(
        label_hot.astype(jnp.bfloat16), class_table, preferred_element_type=jnp.float32
    )
    cond_pre = embedded + sinusoid(tsteps[0], tensor_place * head_cols, head_cols)
    cond_full, silu_back = jax.vjp(jax.nn.silu, cond_pre)
    cond = cond_full.astype(jnp.bfloat16)
    bias_full = lax.dynamic_update_slice_in_dim(
        jnp.zeros((6 * model_width,), jnp.float32), b_mod, tensor_place * bias_len, 0
    )
    mod_partial = jnp.dot(cond, w_mod, preferred_element_type=jnp.float32) + bias_full[None, :]
    modul = lax.psum(mod_partial, "tensor")
    picker = (slot_ids[:, None] == item_ids[None, :]).astype(jnp.float32)
    pick_mine = lax.dynamic_slice_in_dim(picker, tensor_place * my_slots, my_slots, 0)
    per_slot = jnp.dot(pick_mine, modul, precision=lax.Precision.HIGHEST)
    shift_a, scale_a, gate_a, shift_m, scale_m, gate_m = jnp.split(per_slot, 6, axis=1)
    resid = tokens.astype(jnp.float32).reshape(my_slots, SLOT_TOK, model_width)
    normed_one, norm_one_back = jax.vjp(modulated_norm, resid, shift_a, scale_a)
    normed_attn = normed_one.astype(jnp.bfloat16).reshape(local_rows, model_width)
    w_qkv = jnp.concatenate([w_query, w_key, w_value], axis=1)
    attn_all, qkv_lin = fold_rows(w_qkv, lax.all_gather(normed_attn, "tensor", axis=0, tiled=True))
    q_lin, k_lin, v_lin = jnp.split(qkv_lin, 3, axis=1)
    grid_row, grid_col = grid_positions(slot_ids)

    def prepare(query_part, key_part, query_gain, key_gain):
        return (
            head_rotary(query_part, query_gain, grid_row, grid_col),
            head_rotary(key_part, key_gain, grid_row, grid_col),
        )

    (query_full, key_full), prep_back = jax.vjp(prepare, q_lin, k_lin, q_gain, k_gain)
    query_rot = query_full.astype(jnp.bfloat16)
    key_rot = key_full.astype(jnp.bfloat16)
    value_all = v_lin.astype(jnp.bfloat16).reshape(all_rows, local_heads, HEAD_DIM)
    token_items = jnp.repeat(slot_ids, SLOT_TOK).reshape(group_count, group_tok)

    def grouped(array_in):
        return array_in.reshape(group_count, group_tok, local_heads, HEAD_DIM)

    mixed_f, log_totals = lax.map(
        forward_group, (grouped(query_rot), grouped(key_rot), grouped(value_all), token_items)
    )
    mixed = mixed_f.reshape(all_rows, head_cols).astype(jnp.bfloat16)
    attn = (
        lax.psum_scatter(
            rows_times(mixed, w_out, False).astype(jnp.bfloat16),
            "tensor",
            scatter_dimension=0,
            tiled=True,
        )
        .astype(jnp.float32)
        .reshape(resid.shape)
    )
    middle = resid + gate_a[:, None, :] * attn
    normed_two, norm_two_back = jax.vjp(modulated_norm, middle, shift_m, scale_m)
    normed_mlp = normed_two.astype(jnp.bfloat16).reshape(local_rows, model_width)
    w_gate_up = jnp.concatenate([w_gate, w_up], axis=1)
    mlp_all, gate_up_lin = fold_rows(
        w_gate_up, lax.all_gather(normed_mlp, "tensor", axis=0, tiled=True)
    )
    gate_lin, up_lin = jnp.split(gate_up_lin, 2, axis=1)

    def swiglu(gate_part, up_part):
        return jax.nn.silu(gate_part) * up_part

    hidden_f, swiglu_back = jax.vjp(swiglu, gate_lin, up_lin)
    hidden = hidden_f.astype(jnp.bfloat16)
    branch = (
        lax.psum_scatter(
            rows_times(hidden, w_down, False).astype(jnp.bfloat16),
            "tensor",
            scatter_dimension=0,
            tiled=True,
        )
        .astype(jnp.float32)
        .reshape(resid.shape)
    )
    output = (
        (middle + gate_m[:, None, :] * branch).reshape(local_rows, model_width).astype(jnp.bfloat16)
    )
    grad_out = cotangent.astype(jnp.float32).reshape(resid.shape)
    grad_gate_m = jnp.sum(branch * grad_out, axis=1)
    grad_branch = (
        (gate_m[:, None, :] * grad_out).astype(jnp.bfloat16).reshape(local_rows, model_width)
    )
    grad_hidden, grad_w_down = fold_back(
        hidden, w_down, lax.all_gather(grad_branch, "tensor", axis=0, tiled=True)
    )
    grad_gate, grad_up = swiglu_back(grad_hidden)
    grad_gate_up = jnp.concatenate([grad_gate, grad_up], axis=1).astype(jnp.bfloat16)
    grad_w_gate_up = lax.dot_general(
        mlp_all, grad_gate_up, CONTRACT_ROWS, preferred_element_type=jnp.float32
    )
    grad_w_gate, grad_w_up = jnp.split(grad_w_gate_up, 2, axis=1)
    grad_normed_mlp = (
        lax.psum_scatter(
            rows_times(grad_gate_up, w_gate_up, True).astype(jnp.bfloat16),
            "tensor",
            scatter_dimension=0,
            tiled=True,
        )
        .astype(jnp.float32)
        .reshape(resid.shape)
    )
    grad_mid_norm, grad_shift_m, grad_scale_m = norm_two_back(grad_normed_mlp)
    grad_middle = grad_out + grad_mid_norm
    grad_gate_a = jnp.sum(attn * grad_middle, axis=1)
    grad_attn = (
        (gate_a[:, None, :] * grad_middle).astype(jnp.bfloat16).reshape(local_rows, model_width)
    )
    grad_mixed_f, grad_w_out = fold_back(
        mixed, w_out, lax.all_gather(grad_attn, "tensor", axis=0, tiled=True)
    )
    grad_mixed = grad_mixed_f.astype(jnp.bfloat16)
    grad_q_rot, grad_k_rot, grad_v_all = lax.map(
        backward_group,
        (
            grouped(query_rot),
            grouped(key_rot),
            grouped(value_all),
            grouped(grad_mixed),
            log_totals,
            token_items,
        ),
    )
    head_shape = (all_rows, local_heads, HEAD_DIM)
    grad_q_lin, grad_k_lin, grad_q_gain, grad_k_gain = prep_back(
        (grad_q_rot.reshape(head_shape), grad_k_rot.reshape(head_shape))
    )
    grad_qkv = jnp.concatenate(
        [grad_q_lin, grad_k_lin, grad_v_all.reshape(all_rows, head_cols)], axis=1
    ).astype(jnp.bfloat16)
    grad_w_qkv = lax.dot_general(
        attn_all, grad_qkv, CONTRACT_ROWS, preferred_element_type=jnp.float32
    )
    grad_w_query, grad_w_key, grad_w_value = jnp.split(grad_w_qkv, 3, axis=1)
    grad_normed_attn = (
        lax.psum_scatter(
            rows_times(grad_qkv, w_qkv, True).astype(jnp.bfloat16),
            "tensor",
            scatter_dimension=0,
            tiled=True,
        )
        .astype(jnp.float32)
        .reshape(resid.shape)
    )
    grad_resid_norm, grad_shift_a, grad_scale_a = norm_one_back(grad_normed_attn)
    grad_tokens = (
        (grad_middle + grad_resid_norm).reshape(local_rows, model_width).astype(jnp.bfloat16)
    )
    grad_slot = jnp.concatenate(
        [grad_shift_a, grad_scale_a, grad_gate_a, grad_shift_m, grad_scale_m, grad_gate_m], axis=1
    )
    grad_items = lax.dot_general(
        pick_mine,
        grad_slot,
        CONTRACT_ROWS,
        precision=lax.Precision.HIGHEST,
        preferred_element_type=jnp.float32,
    )
    grad_modul, grad_q_gain, grad_k_gain = (
        lax.psum(grad_items.astype(jnp.bfloat16), "tensor").astype(jnp.float32),
        lax.psum(grad_q_gain.astype(jnp.bfloat16), "tensor").astype(jnp.float32),
        lax.psum(grad_k_gain.astype(jnp.bfloat16), "tensor").astype(jnp.float32),
    )
    grad_modul_low = grad_modul.astype(jnp.bfloat16)
    grad_w_mod = lax.dot_general(
        cond, grad_modul_low, CONTRACT_ROWS, preferred_element_type=jnp.float32
    )
    grad_bias_full = jnp.sum(grad_modul_low.astype(jnp.float32), axis=0)
    grad_b_mod = lax.dynamic_slice_in_dim(grad_bias_full, tensor_place * bias_len, bias_len, 0)
    grad_cond = lax.dot_general(
        grad_modul_low, w_mod, CONTRACT_COLS, preferred_element_type=jnp.float32
    )
    grad_cond_pre = silu_back(grad_cond)[0]
    grad_class_table = lax.dot_general(
        label_hot,
        grad_cond_pre,
        CONTRACT_ROWS,
        precision=lax.Precision.HIGHEST,
        preferred_element_type=jnp.float32,
    )
    (
        grad_w_query,
        grad_w_key,
        grad_w_value,
        grad_w_out,
        grad_w_gate,
        grad_w_up,
        grad_w_down,
        grad_w_mod,
        grad_b_mod,
        grad_class_table,
        grad_q_gain,
        grad_k_gain,
    ) = (
        lax.psum(grad_w_query.astype(jnp.bfloat16), "dp").astype(jnp.float32),
        lax.psum(grad_w_key.astype(jnp.bfloat16), "dp").astype(jnp.float32),
        lax.psum(grad_w_value.astype(jnp.bfloat16), "dp").astype(jnp.float32),
        lax.psum(grad_w_out.astype(jnp.bfloat16), "dp").astype(jnp.float32),
        lax.psum(grad_w_gate.astype(jnp.bfloat16), "dp").astype(jnp.float32),
        lax.psum(grad_w_up.astype(jnp.bfloat16), "dp").astype(jnp.float32),
        lax.psum(grad_w_down.astype(jnp.bfloat16), "dp").astype(jnp.float32),
        lax.psum(grad_w_mod.astype(jnp.bfloat16), "dp").astype(jnp.float32),
        lax.psum(grad_b_mod.astype(jnp.bfloat16), "dp").astype(jnp.float32),
        lax.psum(grad_class_table.astype(jnp.bfloat16), "dp").astype(jnp.float32),
        lax.psum(grad_q_gain.astype(jnp.bfloat16), "dp").astype(jnp.float32),
        lax.psum(grad_k_gain.astype(jnp.bfloat16), "dp").astype(jnp.float32),
    )
    return (
        output,
        grad_tokens,
        grad_w_query,
        grad_w_key,
        grad_w_value,
        grad_w_out,
        grad_w_gate,
        grad_w_up,
        grad_w_down,
        grad_w_mod,
        grad_b_mod,
        grad_class_table,
        grad_q_gain,
        grad_k_gain,
    )


def solution(mesh):
    in_specs = (
        P(("dp", "tensor"), None),
        P(None, "tensor"),
        P(None, "tensor"),
        P(None, "tensor"),
        P("tensor", None),
        P(None, "tensor"),
        P(None, "tensor"),
        P("tensor", None),
        P("tensor", None),
        P("tensor"),
        P(None, "tensor"),
        P(),
        P(),
        P("dp", None),
        P("dp", None),
        P("dp", None),
        P(("dp", "tensor"), None),
    )
    out_specs = (
        P(("dp", "tensor"), None),
        P(("dp", "tensor"), None),
        P(None, "tensor"),
        P(None, "tensor"),
        P(None, "tensor"),
        P("tensor", None),
        P(None, "tensor"),
        P(None, "tensor"),
        P("tensor", None),
        P("tensor", None),
        P("tensor"),
        P(None, "tensor"),
        P(),
        P(),
    )
    return jax.shard_map(local, mesh=mesh, in_specs=in_specs, out_specs=out_specs, check_vma=False)
```

profile of v0, /device:TPU:0, one launch (start us, length us, event | category | flops | bytes accessed | tf_op | source)
XLA Modules:
  0.0 817.1 jit_solution(16463656315624647184)
XLA Ops:
  10.9 3.5 convolution_add_fusion
  14.8 32.4 %all-reduce.18.cloned.1.call-done = f32[4,6912]{1,0:T(4,128)} async-done(((f32[4,6912]{1,0:T(4,128)}), f32[4,6912]{1,0:T(4,128)}) %all-reduce.18.cloned.1.call-update) | async-done | bytes 110608 | tf_op jit(solution)/shard_map/psum | solution.py:181
  53.1 1.6 broadcast_compare_fusion
  54.8 21.0 %all-gather.5.cloned.1.call-done = bf16[1024,1152]{1,0:T(8,128)(2,1)} async-done(((bf16[256,1152]{1,0:T(8,128)(2,1)}), bf16[1024,1152]{1,0:T(8,128)(2,1)}) %all-gather.5.cloned.1.call-update) | async-done | bytes 2359312 | tf_op jit(solution)/shard_map/all_gather | solution.py:190
  75.7 4.7 fusion.79
  84.7 8.0 fusion.78
  92.8 8.0 fusion
  100.9 7.5 fusion.19
  108.4 2.9 convolution_convert_fusion.5
  111.4 33.2 %reduce-scatter.5.cloned.1.call-done = bf16[256,1152]{1,0:T(8,128)(2,1)} async-done(((bf16[1024,1152]{1,0:T(8,128)(2,1)}), bf16[256,1152]{1,0:T(8,128)(2,1)}) %reduce-scatter.5.cloned.1.call-update) | async-done | bytes 589840 | tf_op jit(solution)/shard_map/reduce_scatter | solution.py:214
  147.1 1.8 add_convert_fusion
  149.0 1.6 fusion.26
  150.7 2.9 constant_dynamic-update-slice_fusion.4
  154.9 18.2 %all-gather.7.cloned.1.call-done = bf16[1024,1152]{1,0:T(8,128)(2,1)} async-done(((bf16[256,1152]{1,0:T(8,128)(2,1)}), bf16[1024,1152]{1,0:T(8,128)(2,1)}) %all-gather.7.cloned.1.call-update) | async-done | bytes 2359312 | tf_op jit(solution)/shard_map/all_gather | solution.py:228
  173.2 9.6 %fusion.80 = f32[1024,1536]{1,0:T(8,128)} fusion(bf16[1024,1152]{1,0:T(8,128)(2,1)} %all-gather.7.cloned.1.call-done, bf16[1152,1536]{1,0:T(8,128)(2,1)} %constant_dynamic-update-slice_fusion.3), kind=kOutput, calls=%fused_computation.224 | convolution fusion | flops 3623878656 | bytes 12189696 | tf_op jit(solution)/shard_map/dot_general | solution.py:116
  182.8 16.4 %all-gather.9.cloned.1.call-done = bf16[1024,1152]{1,0:T(8,128)(2,1)} async-done(((bf16[256,1152]{1,0:T(8,128)(2,1)}), bf16[1024,1152]{1,0:T(8,128)(2,1)}) %all-gather.9.cloned.1.call-update) | async-done | bytes 2359312 | tf_op jit(solution)/shard_map/all_gather | solution.py:256
  199.2 7.8 fusion.8
  208.7 7.5 convolution_convert_fusion.3
  216.3 33.2 %reduce-scatter.9.cloned.1.call-done = bf16[256,1152]{1,0:T(8,128)(2,1)} async-done(((bf16[1024,1152]{1,0:T(8,128)(2,1)}), bf16[256,1152]{1,0:T(8,128)(2,1)}) %reduce-scatter.9.cloned.1.call-update) | async-done | bytes 589840 | tf_op jit(solution)/shard_map/reduce_scatter | solution.py:265
  253.8 5.0 convolution_convert_fusion.4
  258.9 18.3 %all-gather.11.cloned.1.call-done = bf16[1024,1152]{1,0:T(8,128)(2,1)} async-done(((bf16[256,1152]{1,0:T(8,128)(2,1)}), bf16[1024,1152]{1,0:T(8,128)(2,1)}) %all-gather.11.cloned.1.call-update) | async-done | bytes 2359312 | tf_op jit(solution)/shard_map/all_gather | solution.py:281
  277.2 2.6 convolution_convert_fusion.10
  279.9 15.9 %multiply_reduce_fusion = (f32[4,1024]{1,0:T(4,128)S(1)}, f32[4,1024,1024]{1,2,0:T(8,128)}) fusion(f32[4,1024,1024]{1,2,0:T(8,128)} %get-tuple-element.149, f32[4,1024]{1,0:T(4,128)S(1)} %log_add_fusion, bf16[1024,4,72]{0,2,1:T(8,128)(2,1)S(1)} %bitcast.83, bf16[1024,4,72]{0,2,1:T(8,128)(2,1)S(1)} %bitcast.86), kind=kOutput, calls=%fused_computation.1 | convolution fusion | flops 616558592 | bytes 34766848 | tf_op jit(solution)/shard_map/while/body/eval_jaxpr/qhd,khd->hqk/dot_general | solution.py:100
  297.3 8.1 multiply_convert_fusion
  305.5 1.6 fusion.15
  307.1 1.6 copy-done.2
  310.3 6.1 fusion.14
  321.6 3.0 fusion.16
  324.6 6.0 convolution_convert_fusion.2
  331.3 5.8 convolution_convert_fusion.7
  337.1 4.4 convolution_convert_fusion.1
  341.5 2.1 fusion.75
  344.5 1.8 convolution_convert_fusion.8
  346.4 2.5 convolution_convert_fusion.6
  350.3 13.7 %reduce-scatter.11.cloned.1.call-done = bf16[256,1152]{1,0:T(8,128)(2,1)} async-done(((bf16[1024,1152]{1,0:T(8,128)(2,1)}), bf16[256,1152]{1,0:T(8,128)(2,1)}) %reduce-scatter.11.cloned.1.call-update) | async-done | bytes 589840 | tf_op jit(solution)/shard_map/reduce_scatter | solution.py:307
  364.1 3.8 fusion.28
  368.1 10.7 %all-reduce.14 = (bf16[4,6912]{1,0:T(4,128)(2,1)S(1)}, bf16[72]{0:T(256)(128)(2,1)S(1)}, bf16[72]{0:T(256)(128)(2,1)S(1)}) all-reduce(bf16[4,6912]{1,0:T(4,128)(2,1)S(1)} %multiply_convert_fusion.4, bf16[72]{0:T(256)(128)(2,1)S(1)} %get-tuple-element.57, ...), channel_id=1, replica_groups=mesh['dp'=8,'tensor'=4] {'tensor'}, use_global_device_ids=true, to_apply=%region_31.32 | all-reduce | flops 27792 | bytes 111168 | tf_op jit(solution)/shard_map/psum | solution.py:331
  378.9 3.2 fusion.81
  382.2 3.2 convolution_convert_fusion
  385.4 1.5 convolution_convert_fusion.9
  387.1 22.8 %all-reduce.12 = (bf16[1728]{0:T(1024)(128)(2,1)S(1)}, bf16[72]{0:T(256)(128)(2,1)S(1)}, bf16[72]{0:T(256)(128)(2,1)S(1)}) all-reduce(bf16[1728]{0:T(1024)(128)(2,1)S(1)} %dynamic_slice.38, bf16[72]{0:T(256)(128)(2,1)S(1)} %get-tuple-element.99, bf16[72]{0:T(256)(128)(2,1)S(1)} %get-tuple-element.100), channel_id=1, replica_groups=mesh['dp'=8,'tensor'=4] {'dp'}, use_global_device_ids=true, to_apply=%region_34.35 | all-reduce | flops 1872 | bytes 7488 | tf_op jit(solution)/shard_map/psum | solution.py:374
  411.6 1.7 fusion.33
  413.3 378.4 %all-reduce.20.cloned.1.call-done = (bf16[1152,288]{0,1:T(8,128)(2,1)}, bf16[1152,288]{0,1:T(8,128)(2,1)}, bf16[1152,288]{0,1:T(8,128)(2,1)}, bf16[288,1152]{1,0...) async-done(((bf16[1152,288]{0,1:T(8,128)(2,1)}, ...) | async-done | bytes 12519952 | tf_op jit(solution)/shard_map/psum | solution.py:366
  791.7 2.3 convert_element_type.237
  798.7 2.1 convert_element_type.242
  800.8 2.1 convert_element_type.243
  802.9 2.0 convert_element_type.245
  806.3 3.8 convert_element_type.248
  (313 shorter events, 43.1 us)
Async XLA Ops:
  7.2 192.1 %copy-start = (bf16[768,1152]{1,0:T(8,128)(2,1)S(1)}, bf16[768,1152]{1,0:T(8,128)(2,1)}, u32[]{:S(2)}) copy-start(bf16[768,1152]{1,0:T(8,128)(2,1)} %param.24) | copy-start | bytes 5308420
  7.2 40.0 %all-reduce.18.cloned.1.call-start = ((), (), s32[]{:S(2)}) async-start(), calls=%async_computation.4 | async-start | bytes 221184 | tf_op jit(solution)/shard_map/psum | solution.py:181
  14.4 37.1 %copy-start.49 = (bf16[1152,288]{0,1:T(8,128)(2,1)S(1)}, bf16[1152,288]{0,1:T(8,128)(2,1)}, u32[]{:S(2)}) copy-start(bf16[1152,288]{0,1:T(8,128)(2,1)} %param.18) | copy-start | bytes 1990660
  14.4 61.3 %all-gather.5.cloned.1.call-start = ((), (), s32[]{:S(2)}) async-start(), calls=%async_computation.5 | async-start | bytes 2949120 | tf_op jit(solution)/shard_map/all_gather | solution.py:190
  14.7 32.5 %copy-start.80 = (f32[256]{0:T(256)}, f32[256]{0:T(256)S(1)}, u32[]{:S(2)}) copy-start(f32[256]{0:T(256)S(1)} %fusion.34) | copy-start | bytes 3076
  14.7 36.9 %copy-start.78 = (f32[256]{0:T(256)}, f32[256]{0:T(256)S(1)}, u32[]{:S(2)}) copy-start(f32[256]{0:T(256)S(1)} %fusion.62) | copy-start | bytes 3076
  14.8 32.4 %copy-start.89 = (pred[4,4]{1,0:T(4,128)(4,1)}, pred[4,4]{1,0:T(4,128)(4,1)S(1)}, u32[]{:S(2)}) copy-start(pred[4,4]{1,0:T(4,128)(4,1)S(1)} %iota_compare_fusion.2) | copy-start | bytes 52
  50.1 94.5 %reduce-scatter.5.cloned.1.call-start = ((), (), s32[]{:S(2)}) async-start(), calls=%async_computation.6 | async-start | bytes 2949120 | tf_op jit(solution)/shard_map/reduce_scatter | solution.py:214
  51.5 31.3 %copy-start.15 = (f32[1024,18]{0,1:T(8,128)}, f32[1024,18]{0,1:T(8,128)S(1)}, u32[]{:S(2)}) copy-start(f32[1024,18]{0,1:T(8,128)S(1)} %get-tuple-element.136) | copy-start | bytes 221188
  51.5 31.3 %copy-start.17 = (f32[1024,18]{0,1:T(8,128)}, f32[1024,18]{0,1:T(8,128)S(1)}, u32[]{:S(2)}) copy-start(f32[1024,18]{0,1:T(8,128)S(1)} %get-tuple-element.137) | copy-start | bytes 221188
  51.5 31.3 %copy-start.19 = (f32[1024,18]{0,1:T(8,128)}, f32[1024,18]{0,1:T(8,128)S(1)}, u32[]{:S(2)}) copy-start(f32[1024,18]{0,1:T(8,128)S(1)} %get-tuple-element.142) | copy-start | bytes 221188
  51.6 31.3 %copy-start.21 = (f32[1024,18]{0,1:T(8,128)}, f32[1024,18]{0,1:T(8,128)S(1)}, u32[]{:S(2)}) copy-start(f32[1024,18]{0,1:T(8,128)S(1)} %get-tuple-element.143) | copy-start | bytes 221188
  80.6 20.3 %copy-start.26 = (bf16[1024,288]{0,1:T(8,128)(2,1)}, bf16[1024,288]{0,1:T(8,128)(2,1)S(1)}, u32[]{:S(2)}) copy-start(bf16[1024,288]{0,1:T(8,128)(2,1)S(1)} %split.165) | copy-start | bytes 1769476
  82.9 9.8 %copy-start.33 = (bf16[1024,4,18]{0,2,1:T(8,128)(2,1)}, bf16[1024,4,18]{0,2,1:T(8,128)(2,1)S(1)}, u32[]{:S(2)}) copy-start(bf16[1024,4,18]{0,2,1:T(8,128)(2,1)S(1)} %get-tuple-element.120) | copy-start | bytes 442372
  82.9 9.8 %copy-start.35 = (bf16[1024,4,18]{0,2,1:T(8,128)(2,1)}, bf16[1024,4,18]{0,2,1:T(8,128)(2,1)S(1)}, u32[]{:S(2)}) copy-start(bf16[1024,4,18]{0,2,1:T(8,128)(2,1)S(1)} %get-tuple-element.121) | copy-start | bytes 442372
  82.9 9.8 %copy-start.37 = (bf16[1024,4,18]{0,2,1:T(8,128)(2,1)}, bf16[1024,4,18]{0,2,1:T(8,128)(2,1)S(1)}, u32[]{:S(2)}) copy-start(bf16[1024,4,18]{0,2,1:T(8,128)(2,1)S(1)} %get-tuple-element.132) | copy-start | bytes 442372
  82.9 9.8 %copy-start.39 = (bf16[1024,4,18]{0,2,1:T(8,128)(2,1)}, bf16[1024,4,18]{0,2,1:T(8,128)(2,1)S(1)}, u32[]{:S(2)}) copy-start(bf16[1024,4,18]{0,2,1:T(8,128)(2,1)S(1)} %get-tuple-element.133) | copy-start | bytes 442372
  83.3 9.5 %copy-start.41 = (bf16[1024,4,18]{0,2,1:T(8,128)(2,1)}, bf16[1024,4,18]{0,2,1:T(8,128)(2,1)S(1)}, u32[]{:S(2)}) copy-start(bf16[1024,4,18]{0,2,1:T(8,128)(2,1)S(1)} %get-tuple-element.124) | copy-start | bytes 442372
  83.3 9.5 %copy-start.43 = (bf16[1024,4,18]{0,2,1:T(8,128)(2,1)}, bf16[1024,4,18]{0,2,1:T(8,128)(2,1)S(1)}, u32[]{:S(2)}) copy-start(bf16[1024,4,18]{0,2,1:T(8,128)(2,1)S(1)} %get-tuple-element.125) | copy-start | bytes 442372
  83.3 9.5 %copy-start.45 = (bf16[1024,4,18]{0,2,1:T(8,128)(2,1)}, bf16[1024,4,18]{0,2,1:T(8,128)(2,1)S(1)}, u32[]{:S(2)}) copy-start(bf16[1024,4,18]{0,2,1:T(8,128)(2,1)S(1)} %get-tuple-element.134) | copy-start | bytes 442372
  83.3 9.5 %copy-start.47 = (bf16[1024,4,18]{0,2,1:T(8,128)(2,1)}, bf16[1024,4,18]{0,2,1:T(8,128)(2,1)S(1)}, u32[]{:S(2)}) copy-start(bf16[1024,4,18]{0,2,1:T(8,128)(2,1)S(1)} %get-tuple-element.135) | copy-start | bytes 442372
  111.3 61.8 %all-gather.7.cloned.1.call-start = ((), (), s32[]{:S(2)}) async-start(), calls=%async_computation.7 | async-start | bytes 2949120 | tf_op jit(solution)/shard_map/all_gather | solution.py:228
  148.9 50.3 %all-gather.9.cloned.1.call-start = ((), (), s32[]{:S(2)}) async-start(), calls=%async_computation.9 | async-start | bytes 2949120 | tf_op jit(solution)/shard_map/all_gather | solution.py:256
  150.6 98.8 %reduce-scatter.9.cloned.1.call-start = ((), (), s32[]{:S(2)}) async-start(), calls=%async_computation.10 | async-start | bytes 2949120 | tf_op jit(solution)/shard_map/reduce_scatter | solution.py:265
  216.2 61.0 %all-gather.11.cloned.1.call-start = ((), (), s32[]{:S(2)}) async-start(), calls=%async_computation.11 | async-start | bytes 2949120 | tf_op jit(solution)/shard_map/all_gather | solution.py:281
  253.0 97.3 %reduce-scatter.7.cloned.1.call-start = ((), (), s32[]{:S(2)}) async-start(), calls=%async_computation.8 | async-start | bytes 2949120 | tf_op jit(solution)/shard_map/reduce_scatter | solution.py:238
  258.8 18.4 %copy-start.96 = (bf16[288,1152]{1,0:T(8,128)(2,1)S(1)}, bf16[288,1152]{1,0:T(8,128)(2,1)}, u32[]{:S(2)}) copy-start(bf16[288,1152]{1,0:T(8,128)(2,1)} %param.21) | copy-start | bytes 1990660
  258.8 21.1 %copy-start.27 = (bf16[1024,288]{0,1:T(8,128)(2,1)S(1)}, bf16[1024,288]{0,1:T(8,128)(2,1)}, u32[]{:S(2)}) copy-start(bf16[1024,288]{0,1:T(8,128)(2,1)} %copy-done.26) | copy-start | bytes 1769476
  258.8 105.2 %reduce-scatter.11.cloned.1.call-start = ((), (), s32[]{:S(2)}) async-start(), calls=%async_computation.12 | async-start | bytes 2949120 | tf_op jit(solution)/shard_map/reduce_scatter | solution.py:307
  279.8 16.0 %copy-start.24 = (bf16[1024,288]{0,1:T(8,128)(2,1)}, bf16[1024,288]{0,1:T(8,128)(2,1)S(1)}, u32[]{:S(2)}) copy-start(bf16[1024,288]{0,1:T(8,128)(2,1)S(1)} %convolution_convert_fusion.10) | copy-start | bytes 1769476
  279.9 16.0 %slice-start = ((s8[16777216]{0:T(1024)(128)(4,1)}), s8[4194304]{0:T(1024)(128)(4,1)S(1)}, s32[]{:S(2)}) async-start(s8[16777216]{0:T(1024)(128)(4,1)} %bitcast.73), calls=%async_computation.14 | async-start | bytes 8388608
  279.9 16.0 %slice-start.1 = ((s8[16777216]{0:T(1024)(128)(4,1)}), s8[4194304]{0:T(1024)(128)(4,1)S(1)}, s32[]{:S(2)}) async-start(s8[16777216]{0:T(1024)(128)(4,1)} %bitcast.73), calls=%async_computation.15 | async-start | bytes 8388608
  279.9 16.0 %slice-start.2 = ((s8[16777216]{0:T(1024)(128)(4,1)}), s8[4194304]{0:T(1024)(128)(4,1)S(1)}, s32[]{:S(2)}) async-start(s8[16777216]{0:T(1024)(128)(4,1)} %bitcast.73), calls=%async_computation.16 | async-start | bytes 8388608
  279.9 17.3 %slice-start.3 = ((s8[16777216]{0:T(1024)(128)(4,1)}), s8[4194304]{0:T(1024)(128)(4,1)S(1)}, s32[]{:S(2)}) async-start(s8[16777216]{0:T(1024)(128)(4,1)} %bitcast.73), calls=%async_computation.17 | async-start | bytes 8388608
  297.2 8.2 %copy-start.44 = (bf16[1024,4,18]{0,2,1:T(8,128)(2,1)S(1)}, bf16[1024,4,18]{0,2,1:T(8,128)(2,1)}, u32[]{:S(2)}) copy-start(bf16[1024,4,18]{0,2,1:T(8,128)(2,1)} %copy-done.43) | copy-start | bytes 442372
  297.2 8.2 %copy-start.46 = (bf16[1024,4,18]{0,2,1:T(8,128)(2,1)S(1)}, bf16[1024,4,18]{0,2,1:T(8,128)(2,1)}, u32[]{:S(2)}) copy-start(bf16[1024,4,18]{0,2,1:T(8,128)(2,1)} %copy-done.45) | copy-start | bytes 442372
  297.2 8.2 %copy-start.48 = (bf16[1024,4,18]{0,2,1:T(8,128)(2,1)S(1)}, bf16[1024,4,18]{0,2,1:T(8,128)(2,1)}, u32[]{:S(2)}) copy-start(bf16[1024,4,18]{0,2,1:T(8,128)(2,1)} %copy-done.47) | copy-start | bytes 442372
  330.7 461.0 %all-reduce.20.cloned.1.call-start = ((), (), s32[]{:S(2)}) async-start(), calls=%async_computation.13 | async-start | bytes 25067520 | tf_op jit(solution)/shard_map/psum | solution.py:366
  348.9 15.2 %copy-start.9 = (bf16[256,1152]{1,0:T(8,128)(2,1)S(1)}, bf16[256,1152]{1,0:T(8,128)(2,1)}, u32[]{:S(2)}) copy-start(bf16[256,1152]{1,0:T(8,128)(2,1)} %reduce-scatter.5.cloned.1.call-done) | copy-start | bytes 1769476
  348.9 15.2 %copy-start.11 = (bf16[256,1152]{1,0:T(8,128)(2,1)S(1)}, bf16[256,1152]{1,0:T(8,128)(2,1)}, u32[]{:S(2)}) copy-start(bf16[256,1152]{1,0:T(8,128)(2,1)} %reduce-scatter.9.cloned.1.call-done) | copy-start | bytes 1769476
  348.9 15.1 %copy-start.13 = (bf16[256,1152]{1,0:T(8,128)(2,1)S(1)}, bf16[256,1152]{1,0:T(8,128)(2,1)}, u32[]{:S(2)}) copy-start(bf16[256,1152]{1,0:T(8,128)(2,1)} %param.33) | copy-start | bytes 1769476
  348.9 15.1 %copy-start.67 = (f32[1152]{0:T(1024)S(1)}, f32[1152]{0:T(1024)}, u32[]{:S(2)}) copy-start(f32[1152]{0:T(1024)} %copy-done.66) | copy-start | bytes 13828
  348.9 15.1 %copy-start.68 = (f32[1152]{0:T(1024)S(1)}, f32[1152]{0:T(1024)}, u32[]{:S(2)}) copy-start(f32[1152]{0:T(1024)} %get-tuple-element.78) | copy-start | bytes 13828
  348.9 15.1 %copy-start.75 = (f32[256]{0:T(256)S(1)}, f32[256]{0:T(256)}, u32[]{:S(2)}) copy-start(f32[256]{0:T(256)} %copy-done.73) | copy-start | bytes 3076
  348.9 15.1 %copy-start.77 = (f32[256]{0:T(256)S(1)}, f32[256]{0:T(256)}, u32[]{:S(2)}) copy-start(f32[256]{0:T(256)} %copy-done.76) | copy-start | bytes 3076
  348.9 15.1 %copy-start.79 = (f32[256]{0:T(256)S(1)}, f32[256]{0:T(256)}, u32[]{:S(2)}) copy-start(f32[256]{0:T(256)} %copy-done.78) | copy-start | bytes 3076
  386.9 24.7 %copy-start.81 = (f32[256]{0:T(256)S(1)}, f32[256]{0:T(256)}, u32[]{:S(2)}) copy-start(f32[256]{0:T(256)} %copy-done.80) | copy-start | bytes 3076
  386.9 24.7 %copy-start.23 = (bf16[256,1152]{1,0:T(8,128)(2,1)S(1)}, bf16[256,1152]{1,0:T(8,128)(2,1)}, u32[]{:S(2)}) copy-start(bf16[256,1152]{1,0:T(8,128)(2,1)} %reduce-scatter.11.cloned.1.call-done) | copy-start | bytes 1769476
  (69 other events, 169.0 us)
Sparse Core Ops, SparseCore 0:
  14.5 32.5 all-reduce.17
  50.2 25.5 all-gather.4
  111.4 33.0 reduce-scatter.4
  149.0 24.0 all-gather.6
  175.1 24.0 all-gather.8
  216.4 33.0 reduce-scatter.8
  253.1 24.0 all-gather.10
  280.5 33.0 reduce-scatter.6
  330.8 33.1 reduce-scatter.10
  387.1 404.6 all-reduce.19
where the time goes:
time: 824 us; the launch traced here: 817 us
  waiting for transfers between devices  565 us (69%)
  matrix products  117 us (14%)
  other arithmetic  59.4 us (7%)
  blocking collectives  33.6 us (4%)
  local copies, waits for them, and re-layouts  26.3 us (3%)
  between operations  15.7 us (2%)
    psum x1, waiting for transfers between devices, local(): lax.psum(grad_w_query.astype(jnp.bfloat16), 'dp').astype(jnp.float32)  378 us
    reduce_scatter x1, waiting for transfers between devices, local(): lax.psum_scatter(rows_times(mixed, w_out, False).astype(jnp.bfloat16), 't...  33.2 us
    reduce_scatter x1, waiting for transfers between devices, local(): lax.psum_scatter(rows_times(grad_gate_up, w_gate_up, True).astype(jnp.bfl...  33.2 us
    psum x1, waiting for transfers between devices, local(): modul = lax.psum(mod_partial, 'tensor')  32.4 us
    psum x1, blocking collectives, local(): lax.psum(grad_b_mod.astype(jnp.bfloat16), 'dp').astype(jnp.float32)  22.8 us
    all_gather x1, waiting for transfers between devices, local(): lax.all_gather(normed_attn, 'tensor', axis=0, tiled=True)  21 us
    unnamed x229, local copies, waits for them, and re-layouts  20.1 us
    all_gather x1, waiting for transfers between devices, local(): lax.all_gather(grad_attn, 'tensor', axis=0, tiled=True)  18.3 us
  transfers between devices with their start and end apart: 10, of which 9 were waited for; matrix products, arithmetic and copies ran while one was open for 11% of the time, Pallas kernels for 0%

commit v1 on v0

v1 whole, which is shorter than its diff:
```python
import math

import jax
import jax.numpy as jnp
from jax import lax
from jax.sharding import PartitionSpec as P

D = 1152
HEAD_DIM = 72
SIDE = 16
SLOT_TOK = 256


EPSILON = 1e-06
MASKED = -1000000000.0
CONTRACT_ROWS = (((0,), (0,)), ((), ()))
CONTRACT_COLS = (((1,), (1,)), ((), ()))


def sinusoid(step_ids, first_col, col_count):
    half_width = D // 2
    feature = first_col + jnp.arange(col_count, dtype=jnp.int32)
    freq_index = (feature % half_width).astype(jnp.float32)
    rates = jnp.exp(-math.log(10000.0) * freq_index / half_width)
    angles = step_ids.astype(jnp.float32)[:, None] * rates[None, :]
    return jnp.where(feature[None, :] < half_width, jnp.cos(angles), jnp.sin(angles))


def grid_positions(slot_ids):
    slot_count = slot_ids.shape[0]
    slot_order = jnp.arange(slot_count, dtype=jnp.int32)
    same_item = (slot_ids[:, None] == slot_ids[None, :]) & (slot_ids[:, None] >= 0)
    members = jnp.sum(same_item.astype(jnp.int32), axis=1)
    first_slot = jnp.min(jnp.where(same_item, slot_order[None, :], slot_count), axis=1)
    first_slot = jnp.where(members > 0, first_slot, slot_order)
    side_len = jnp.where(members > 1, 2 * SIDE, SIDE)
    within = jnp.arange(SLOT_TOK, dtype=jnp.int32)
    place_in = (slot_order - first_slot)[:, None] * SLOT_TOK + within[None, :]
    return ((place_in // side_len[:, None]).reshape(-1), (place_in % side_len[:, None]).reshape(-1))


def turn_half(values, grid_index):
    half_len = values.shape[-1] // 2
    rates = jnp.exp(-math.log(10000.0) * jnp.arange(half_len, dtype=jnp.float32) / half_len)
    angles = grid_index.astype(jnp.float32)[:, None] * rates[None, :]
    cosine = jnp.cos(angles)[:, None, :]
    sine_v = jnp.sin(angles)[:, None, :]
    front = values[..., :half_len]
    back_half = values[..., half_len:]
    return jnp.concatenate(
        [front * cosine - back_half * sine_v, back_half * cosine + front * sine_v], axis=-1
    )


def head_rotary(linear, head_gain, grid_row, grid_col):
    per_head = linear.reshape(linear.shape[0], -1, HEAD_DIM)
    normed = (
        per_head
        * lax.rsqrt(jnp.mean(per_head * per_head, axis=-1, keepdims=True) + EPSILON)
        * head_gain
    )
    half_dim = HEAD_DIM // 2
    return jnp.concatenate(
        [turn_half(normed[..., :half_dim], grid_row), turn_half(normed[..., half_dim:], grid_col)],
        axis=-1,
    )


def modulated_norm(values, shift_by, scale_by):
    normed = values * lax.rsqrt(jnp.mean(values * values, axis=-1, keepdims=True) + EPSILON)
    return normed * (1.0 + scale_by[:, None, :]) + shift_by[:, None, :]


def masked_scores(query_blk, key_blk, item_of):
    raw_scores = jnp.einsum(
        "qhd,khd->hqk", query_blk, key_blk, preferred_element_type=jnp.float32
    ) * (1.0 / math.sqrt(HEAD_DIM))
    allowed = item_of[:, None] == item_of[None, :]
    return jnp.where(allowed[None], raw_scores, MASKED)


def forward_group(group_args):
    query_blk, key_blk, value_blk, item_of = group_args
    scores = masked_scores(query_blk, key_blk, item_of)
    row_max = jnp.max(scores, axis=-1, keepdims=True)
    weights_exp = jnp.exp(scores - row_max)
    row_total = jnp.sum(weights_exp, axis=-1, keepdims=True)
    probs_low = (weights_exp / row_total).astype(jnp.bfloat16)
    mixed_blk = jnp.einsum("hqk,khd->qhd", probs_low, value_blk, preferred_element_type=jnp.float32)
    return (mixed_blk, (row_max + jnp.log(row_total))[..., 0])


def backward_group(group_args):
    query_blk, key_blk, value_blk, grad_blk, log_total, item_of = group_args
    scores = masked_scores(query_blk, key_blk, item_of)
    probs = jnp.exp(scores - log_total[..., None])
    grad_value = jnp.einsum(
        "hqk,qhd->khd", probs.astype(jnp.bfloat16), grad_blk, preferred_element_type=jnp.float32
    )
    grad_probs = jnp.einsum("qhd,khd->hqk", grad_blk, value_blk, preferred_element_type=jnp.float32)
    row_dot = jnp.sum(probs * grad_probs, axis=-1, keepdims=True)
    grad_scores = (probs * (grad_probs - row_dot)).astype(jnp.bfloat16)
    inv_root = 1.0 / math.sqrt(HEAD_DIM)
    grad_query = (
        jnp.einsum("hqk,khd->qhd", grad_scores, key_blk, preferred_element_type=jnp.float32)
        * inv_root
    )
    grad_key = (
        jnp.einsum("hqk,qhd->khd", grad_scores, query_blk, preferred_element_type=jnp.float32)
        * inv_root
    )
    return (grad_query, grad_key, grad_value)


def swap(values, axis_name, bit):
    count = lax.axis_size(axis_name)
    return lax.ppermute(values, axis_name, [(i, i ^ bit) for i in range(count)])


def gather_rows(own):
    near = swap(own, "tensor", 1)
    far = swap(own, "tensor", 2)
    diag = swap(far, "tensor", 1)
    return jnp.concatenate([own, near, far, diag], axis=0)


def scatter_rows(partials):
    far_keep, far_send = partials[2], partials[3]
    far_sum = far_keep.astype(jnp.float32) + swap(far_send, "tensor", 1).astype(jnp.float32)
    far_got = swap(far_sum.astype(jnp.bfloat16), "tensor", 2)
    near_sum = partials[0].astype(jnp.float32) + swap(partials[1], "tensor", 1).astype(jnp.float32)
    return near_sum + far_got.astype(jnp.float32)


def bits_of(axis_name):
    count = lax.axis_size(axis_name)
    bits = []
    bit = 1
    while bit < count:
        bits.append(bit)
        bit *= 2
    assert bit == count
    return bits


def gather_dp(values):
    for bit in reversed(bits_of("dp")):
        values = jnp.concatenate([values, swap(values, "dp", bit)], axis=0)
    return values


def reduce_dp(grad, bits):
    place = lax.axis_index("dp")
    low = grad.astype(jnp.bfloat16)
    for bit in bits:
        half = low.shape[0] // 2
        upper = (place // bit) % 2
        mine = lax.dynamic_slice_in_dim(low, upper * half, half, 0)
        other = lax.dynamic_slice_in_dim(low, (1 - upper) * half, half, 0)
        low = (mine.astype(jnp.float32) + swap(other, "dp", bit).astype(jnp.float32)).astype(
            jnp.bfloat16
        )
    for bit in reversed(bits):
        upper = (place // bit) % 2
        got = swap(low, "dp", bit)
        low = jnp.where(
            upper == 1,
            jnp.concatenate([got, low], axis=0),
            jnp.concatenate([low, got], axis=0),
        )
    return low.astype(jnp.float32)


def rows_dot(source, weight):
    return jnp.dot(source, weight, preferred_element_type=jnp.float32)


def dot_cols(source, weight):
    return lax.dot_general(source, weight, CONTRACT_COLS, preferred_element_type=jnp.float32)


def dot_rows(left, right):
    return lax.dot_general(left, right, CONTRACT_ROWS, preferred_element_type=jnp.float32)


def slot_parts(rows_fn, source):
    far = rows_fn(source[2 * SLOT_TOK :]).astype(jnp.bfloat16)
    near = rows_fn(source[: 2 * SLOT_TOK]).astype(jnp.bfloat16)
    return [near[:SLOT_TOK], near[SLOT_TOK:], far[:SLOT_TOK], far[SLOT_TOK:]]


def local(
    tokens,
    w_query,
    w_key,
    w_value,
    w_out,
    w_gate,
    w_up,
    w_down,
    w_mod,
    b_mod,
    class_table,
    q_gain,
    k_gain,
    slot_item,
    labels,
    tsteps,
    cotangent,
):
    tensor_count = lax.axis_size("tensor")
    tensor_place = lax.axis_index("tensor")
    slot_count = slot_item.shape[1]
    assert tensor_count == 4 and slot_count == 4
    local_rows = tokens.shape[0]
    model_width = tokens.shape[1]
    all_rows = local_rows * tensor_count
    head_cols = w_query.shape[1]
    local_heads = head_cols // HEAD_DIM
    bias_len = b_mod.shape[0]
    item_count = labels.shape[1]
    slot_ids = slot_item[0]
    rel_slots = tensor_place ^ jnp.arange(slot_count, dtype=jnp.int32)

    tokens_all = gather_rows(tokens)

    ids_all = gather_dp(jnp.stack([labels[0], tsteps[0]], axis=1))
    item_ids = jnp.arange(item_count, dtype=jnp.int32)
    class_ids = jnp.arange(class_table.shape[0], dtype=jnp.int32)

    def condition(label_ids, step_ids):
        label_hot = (label_ids[:, None] == class_ids[None, :]).astype(jnp.float32)
        embedded = jnp.dot(
            label_hot.astype(jnp.bfloat16), class_table, preferred_element_type=jnp.float32
        )
        cond_pre = embedded + sinusoid(step_ids, tensor_place * head_cols, head_cols)
        return label_hot, cond_pre

    _, cond_own = condition(labels[0], tsteps[0])
    cond_low = jax.nn.silu(cond_own).astype(jnp.bfloat16)
    bias_full = lax.dynamic_update_slice_in_dim(
        jnp.zeros((6 * model_width,), jnp.float32), b_mod, tensor_place * bias_len, 0
    )
    modul = jnp.dot(cond_low, w_mod, preferred_element_type=jnp.float32) + bias_full[None, :]
    modul = modul + swap(modul, "tensor", 1)
    modul = modul + swap(modul, "tensor", 2)
    picker = (slot_ids[:, None] == item_ids[None, :]).astype(jnp.float32)
    rel_hot = (rel_slots[:, None] == jnp.arange(slot_count, dtype=jnp.int32)[None, :]).astype(
        jnp.float32
    )
    rel_pick = jnp.dot(rel_hot, picker, precision=lax.Precision.HIGHEST)
    per_slot = jnp.dot(rel_pick, modul, precision=lax.Precision.HIGHEST)
    shift_a_all, scale_a_all = per_slot[:, :model_width], per_slot[:, model_width : 2 * model_width]
    shift_a, scale_a, gate_a, shift_m, scale_m, gate_m = jnp.split(per_slot[:1], 6, axis=1)

    grad_out = cotangent.astype(jnp.float32)
    grad_branch = gather_rows((gate_m * grad_out).astype(jnp.bfloat16))

    resid = tokens.astype(jnp.float32)
    attn_all = (
        modulated_norm(
            tokens_all.astype(jnp.float32).reshape(slot_count, SLOT_TOK, model_width),
            shift_a_all,
            scale_a_all,
        )
        .astype(jnp.bfloat16)
        .reshape(all_rows, model_width)
    )
    w_qkv = jnp.concatenate([w_query, w_key, w_value], axis=1)
    qkv_lin = rows_dot(attn_all, w_qkv)
    q_lin, k_lin, v_lin = jnp.split(qkv_lin, 3, axis=1)
    rel_int = rel_hot.astype(jnp.int32)
    grid_row, grid_col = grid_positions(slot_ids)

    def rel_tokens(per_token):
        return jnp.sum(
            rel_int[:, :, None] * per_token.reshape(1, slot_count, SLOT_TOK), axis=1
        ).reshape(-1)

    grid_row, grid_col = rel_tokens(grid_row), rel_tokens(grid_col)
    token_items = rel_tokens(jnp.repeat(slot_ids, SLOT_TOK))

    def prepare(query_part, key_part, query_gain, key_gain):
        return (
            head_rotary(query_part, query_gain, grid_row, grid_col),
            head_rotary(key_part, key_gain, grid_row, grid_col),
        )

    (query_full, key_full), prep_back = jax.vjp(prepare, q_lin, k_lin, q_gain, k_gain)
    query_rot = query_full.astype(jnp.bfloat16)
    key_rot = key_full.astype(jnp.bfloat16)
    value_all = v_lin.astype(jnp.bfloat16).reshape(all_rows, local_heads, HEAD_DIM)
    mixed_f, log_totals = forward_group((query_rot, key_rot, value_all, token_items))
    mixed = mixed_f.reshape(all_rows, head_cols).astype(jnp.bfloat16)
    attn = scatter_rows(slot_parts(lambda rows: rows_dot(rows, w_out), mixed))
    middle = resid + gate_a * attn

    def norm_rows(values, shift_by, scale_by):
        return modulated_norm(values[None], shift_by, scale_by)[0]

    normed_two, norm_two_back = jax.vjp(norm_rows, middle, shift_m, scale_m)
    mlp_all = gather_rows(normed_two.astype(jnp.bfloat16))
    w_gate_up = jnp.concatenate([w_gate, w_up], axis=1)
    gate_up_lin = rows_dot(mlp_all, w_gate_up)
    gate_lin, up_lin = jnp.split(gate_up_lin, 2, axis=1)

    def swiglu(gate_part, up_part):
        return jax.nn.silu(gate_part) * up_part

    hidden_f, swiglu_back = jax.vjp(swiglu, gate_lin, up_lin)
    hidden = hidden_f.astype(jnp.bfloat16)
    grad_gate, grad_up = swiglu_back(dot_cols(grad_branch, w_down))
    grad_gate_up = jnp.concatenate([grad_gate, grad_up], axis=1).astype(jnp.bfloat16)
    grad_normed_mlp = scatter_rows(slot_parts(lambda rows: dot_cols(rows, w_gate_up), grad_gate_up))
    grad_w_gate_up = reduce_dp(dot_rows(mlp_all, grad_gate_up), bits_of("dp"))
    grad_w_down = reduce_dp(dot_rows(hidden, grad_branch), bits_of("dp")[1:] + [1])
    grad_w_gate, grad_w_up = jnp.split(grad_w_gate_up, 2, axis=1)

    branch = scatter_rows(slot_parts(lambda rows: rows_dot(rows, w_down), hidden))
    output = (middle + gate_m * branch).astype(jnp.bfloat16)
    grad_gate_m = jnp.sum(branch * grad_out, axis=0, keepdims=True)

    grad_mid_norm, grad_shift_m, grad_scale_m = norm_two_back(grad_normed_mlp)
    grad_middle = grad_out + grad_mid_norm
    grad_gate_a = jnp.sum(attn * grad_middle, axis=0, keepdims=True)
    grad_attn = gather_rows((gate_a * grad_middle).astype(jnp.bfloat16))
    grad_mixed = dot_cols(grad_attn, w_out).astype(jnp.bfloat16)
    grad_w_out = reduce_dp(dot_rows(mixed, grad_attn), bits_of("dp"))
    grad_q_rot, grad_k_rot, grad_v_all = backward_group(
        (
            query_rot,
            key_rot,
            value_all,
            grad_mixed.reshape(all_rows, local_heads, HEAD_DIM),
            log_totals,
            token_items,
        )
    )
    grad_q_lin, grad_k_lin, grad_q_gain, grad_k_gain = prep_back((grad_q_rot, grad_k_rot))
    grad_qkv = jnp.concatenate(
        [grad_q_lin, grad_k_lin, grad_v_all.reshape(all_rows, head_cols)], axis=1
    ).astype(jnp.bfloat16)
    grad_normed_attn = scatter_rows(slot_parts(lambda rows: dot_cols(rows, w_qkv), grad_qkv))
    grad_w_qkv = reduce_dp(dot_rows(attn_all, grad_qkv), bits_of("dp"))
    grad_w_query, grad_w_key, grad_w_value = jnp.split(grad_w_qkv, 3, axis=1)
    _, norm_one_back = jax.vjp(norm_rows, resid, shift_a, scale_a)
    grad_resid_norm, grad_shift_a, grad_scale_a = norm_one_back(grad_normed_attn)
    grad_tokens = (grad_middle + grad_resid_norm).astype(jnp.bfloat16)

    grad_slot = jnp.concatenate(
        [
            grad_shift_a,
            grad_scale_a,
            grad_gate_a,
            grad_shift_m,
            grad_scale_m,
            grad_gate_m,
            grad_q_gain[None],
            grad_k_gain[None],
        ],
        axis=1,
    )
    grad_slots = gather_rows(grad_slot)
    mod_width = 6 * model_width
    grad_items = lax.dot_general(
        rel_pick,
        grad_slots[:, :mod_width],
        CONTRACT_ROWS,
        precision=lax.Precision.HIGHEST,
        preferred_element_type=jnp.float32,
    ).astype(jnp.bfloat16)
    gain_sum = jnp.sum(grad_slots[:, mod_width:], axis=0, keepdims=True)
    gain_rows = jnp.concatenate(
        [gain_sum, jnp.zeros((item_count - 1, gain_sum.shape[1]), jnp.float32)], axis=0
    )
    items_all = gather_dp(jnp.concatenate([grad_items, gain_rows.astype(jnp.bfloat16)], axis=1))
    grad_modul_low = items_all[:, :mod_width]
    gains = jnp.sum(items_all[:, mod_width:].astype(jnp.float32), axis=0)
    grad_q_gain, grad_k_gain = gains[:HEAD_DIM], gains[HEAD_DIM:]
    label_hot, cond_pre = condition(ids_all[:, 0], ids_all[:, 1])
    cond_full, silu_back = jax.vjp(jax.nn.silu, cond_pre)
    grad_w_mod = dot_rows(cond_full.astype(jnp.bfloat16), grad_modul_low)
    grad_bias_full = jnp.sum(grad_modul_low.astype(jnp.float32), axis=0)
    grad_b_mod = lax.dynamic_slice_in_dim(grad_bias_full, tensor_place * bias_len, bias_len, 0)
    grad_cond_pre = silu_back(dot_cols(grad_modul_low, w_mod))[0]
    grad_class_table = lax.dot_general(
        label_hot,
        grad_cond_pre,
        CONTRACT_ROWS,
        precision=lax.Precision.HIGHEST,
        preferred_element_type=jnp.float32,
    )
    return (
        output,
        grad_tokens,
        grad_w_query,
        grad_w_key,
        grad_w_value,
        grad_w_out,
        grad_w_gate,
        grad_w_up,
        grad_w_down,
        grad_w_mod,
        grad_b_mod,
        grad_class_table,
        grad_q_gain,
        grad_k_gain,
    )


def solution(mesh):
    in_specs = (
        P(("dp", "tensor"), None),
        P(None, "tensor"),
        P(None, "tensor"),
        P(None, "tensor"),
        P("tensor", None),
        P(None, "tensor"),
        P(None, "tensor"),
        P("tensor", None),
        P("tensor", None),
        P("tensor"),
        P(None, "tensor"),
        P(),
        P(),
        P("dp", None),
        P("dp", None),
        P("dp", None),
        P(("dp", "tensor"), None),
    )
    out_specs = (
        P(("dp", "tensor"), None),
        P(("dp", "tensor"), None),
        P(None, "tensor"),
        P(None, "tensor"),
        P(None, "tensor"),
        P("tensor", None),
        P(None, "tensor"),
        P(None, "tensor"),
        P("tensor", None),
        P("tensor", None),
        P("tensor"),
        P(None, "tensor"),
        P(),
        P(),
    )
    return jax.shard_map(local, mesh=mesh, in_specs=in_specs, out_specs=out_specs, check_vma=False)
```

time: 824 us -> 512 us (0.62)
  waiting for transfers between devices: 565 us -> 231 us
  starting transfers between devices: 0.42 us -> 50.4 us
  blocking collectives: 33.6 us -> 0 us
  matrix products: 117 us -> 93.3 us
  other arithmetic: 59.4 us -> 80.5 us
  local copies, waits for them, and re-layouts: 26.3 us -> 44.1 us
  between operations: 15.7 us -> 3.12 us
    psum x2 -> x0, waiting for transfers between devices: 411 us -> none  [the longest x1 378 us: local(): lax.psum(grad_w_query.astype(jnp.bfloat16), 'dp').astype(jnp.float32)]
    ppermute x0 -> x59, waiting for transfers between devices: none -> 231 us  [swap(): return lax.ppermute(values, axis_name, [(i, i ^ bit) for i in range(count)])]
    reduce_scatter x4 -> x0, waiting for transfers between devices: 80.1 us -> none  [the longest x1 33.2 us: local(): lax.psum_scatter(rows_times(mixed, w_out, False).astype(jnp.bfloat16), 't...]
    all_gather x4 -> x0, waiting for transfers between devices: 74 us -> none  [the longest x1 21 us: local(): lax.all_gather(normed_attn, 'tensor', axis=0, tiled=True)]
    ppermute x0 -> x59, starting transfers between devices: none -> 50.4 us  [swap(): return lax.ppermute(values, axis_name, [(i, i ^ bit) for i in range(count)])]
    psum x2 -> x0, blocking collectives: 33.6 us -> none  [the longest x1 22.8 us: local(): lax.psum(grad_b_mod.astype(jnp.bfloat16), 'dp').astype(jnp.float32)]
    dot_general x17 -> x23, matrix products: 73.1 us -> 57 us  [the longest x7 20.2 us: dot_cols(): lax.dot_general(source, weight, CONTRACT_COLS, preferred_element_type=jnp...]
    select_n x0 -> x10, other arithmetic: none -> 8.79 us  [the longest x8 8.51 us: reduce_dp(): jnp.where(upper == 1, jnp.concatenate([got, low], axis=0), jnp.concatenat...]
  transfers between devices with their start and end apart: 10 -> 59, of which waited for: 9 -> 26; matrix products, arithmetic and copies ran while one was open for 11% -> 30% of each run, Pallas kernels for 0% -> 0%
where the time goes in v1:
time: 512 us; the launch traced here: 503 us
  waiting for transfers between devices  231 us (45%)
  matrix products  93.3 us (18%)
  other arithmetic  80.5 us (16%)
  starting transfers between devices  50.4 us (10%)
  local copies, waits for them, and re-layouts  44.1 us (9%)
    ppermute x59, waiting for transfers between devices, swap(): return lax.ppermute(values, axis_name, [(i, i ^ bit) for i in range(count)])  231 us
    ppermute x59, starting transfers between devices, swap(): return lax.ppermute(values, axis_name, [(i, i ^ bit) for i in range(count)])  50.4 us
    dot_general x7, matrix products, dot_cols(): lax.dot_general(source, weight, CONTRACT_COLS, preferred_element_type=jnp...  20.2 us
    dot_general x5, matrix products, dot_rows(): lax.dot_general(left, right, CONTRACT_ROWS, preferred_element_type=jnp.fl...  16.6 us
    unnamed x258, local copies, waits for them, and re-layouts  13.2 us
    dot_general x6, matrix products, rows_dot(): return jnp.dot(source, weight, preferred_element_type=jnp.float32)  13.2 us
    convert_element_type x4, other arithmetic, reduce_dp(): return low.astype(jnp.float32)  12.1 us
    convert_element_type x1, other arithmetic, backward_group(): grad_scores = (probs * (grad_probs - row_dot)).astype(jnp.bfloat16)  11.1 us
  transfers between devices with their start and end apart: 59, of which 26 were waited for; matrix products, arithmetic and copies ran while one was open for 30% of the time, Pallas kernels for 0%

profile of v1, /device:TPU:0, one launch (start us, length us, event | category | flops | bytes accessed | tf_op | source)
XLA Modules:
  0.0 502.5 jit_solution(13482286978483217226)
XLA Ops:
  1.2 2.6 collective-permute-start.3
  5.3 4.2 convolution_add_fusion
  14.8 3.3 collective-permute-done.3
  21.2 4.8 fusion.9
  31.5 8.2 %fusion.115 = (f32[4,1024]{1,0:T(4,128)S(1)}, f32[4,1024,1024]{1,2,0:T(8,128)}) fusion(bf16[1024,4,18]{0,2,1:T(8,128)(2,1)S(1)} %get-tuple-element.74, bf16[1024,4,18]{0,2,1:T(8,128)(2,1)S(1)} %get-tuple-element.75, bf16[1024,4,18]{0,2,1:T(8,128)(2,1)S(1)} %get-tuple-element.65, bf16[1024,4,18]{0,2,1:T(8,128)(2,1)S(1)} %get-tuple-element.64, ...), kind=kOutput, calls=%fused_computation.323 | convolution fusion | flops 621277184 | bytes 19021824 | tf_op jit(solution)/shard_map/qhd,khd->hqk/dot_general | solution.py:75
  39.7 8.0 %fusion = f32[4,1024]{1,0:T(4,128)S(1)} fusion(f32[4,1024,1024]{1,2,0:T(8,128)} %get-tuple-element.98, f32[4,1024]{1,0:T(4,128)S(1)} %get-tuple-element.97), kind=kLoop, calls=%fused_computation.6 | loop fusion | flops 8384512 | bytes 16809984 | tf_op jit(solution)/shard_map/reduce_sum | solution.py:87
  47.8 7.5 %fusion.26 = bf16[4,72,1024]{2,1,0:T(8,128)(2,1)S(1)} fusion(bf16[1024,4,72]{0,2,1:T(8,128)(2,1)S(1)} %bitcast.91, f32[4,1024,1024]{1,2,0:T(8,128)} %get-tuple-element.98, f32[4,1024]{1,0:T(4,128)S(1)} %fusion, f32[4,1024]{1,0:T(4,128)S(1)} %get-tuple-element.97), kind=kOutput, calls=%fused_computation.82 | convolution fusion | flops 616857600 | bytes 17989632 | tf_op jit(solution)/shard_map/hqk,khd->qhd/dot_general | solution.py:89
  56.9 2.9 collective-permute-start.50
  66.5 2.9 constant_dynamic-update-slice_fusion.3
  72.5 6.9 %collective-permute-done.7 = bf16[256,1152]{1,0:T(8,128)(2,1)S(1)} collective-permute-done((bf16[256,1152]{1,0:T(8,128)(2,1)}, bf16[256,1152]{1,0:T(8,128)(2,1)S(1)}, u32[]{:S(2)}, u32[]{:S(2)}) %collective-permute-start.7) | collective-permute-done | bytes 589856 | tf_op jit(solution)/shard_map/ppermute | solution.py:117
  92.0 8.3 %collective-permute-done.9 = bf16[256,1152]{1,0:T(8,128)(2,1)} collective-permute-done((bf16[256,1152]{1,0:T(8,128)(2,1)}, bf16[256,1152]{1,0:T(8,128)(2,1)}, u32[]{:S(2)}, u32[]{:S(2)}) %collective-permute-start.9) | collective-permute-done | bytes 589856 | tf_op jit(solution)/shard_map/ppermute | solution.py:117
  102.8 8.6 %collective-permute-done.15 = bf16[256,1152]{1,0:T(8,128)(2,1)} collective-permute-done((bf16[256,1152]{1,0:T(8,128)(2,1)}, bf16[256,1152]{1,0:T(8,128)(2,1)}, u32[]{:S(2)}, u32[]{:S(2)}) %collective-permute-start.15) | collective-permute-done | bytes 589856 | tf_op jit(solution)/shard_map/ppermute | solution.py:117
  112.2 6.6 %fusion.43 = f32[1024,1536]{1,0:T(8,128)S(1)} fusion(bf16[1152,1536]{1,0:T(8,128)(2,1)} %constant_dynamic-update-slice_fusion.3, bf16[256,1152]{1,0:T(8,128)(2,1)S(1)} %collective-permute-done.10, bf16[256,1152]{1,0:T(8,128)(2,1)} %collective-permute-done.9, bf16[256,1152]{1,0:T(8,128)(2,1)S(1)} %collective-permute-done.8, ...), kind=kOutput, calls=%fused_computation.146 | convolution fusion | flops 3633315840 | bytes 12189696 | tf_op jit(solution)/shard_map/dot_general | solution.py:175
  118.8 6.2 %multiply_convert_fusion.1 = (bf16[1024,768]{1,0:T(8,128)(2,1)S(1)}, bf16[1024,768]{1,0:T(8,128)(2,1)S(1)}, bf16[1024,768]{1,0:T(8,128)(2,1)S(1)}) fusion(f32[1024,1536]{1,0:T(8,128)S(1)} %fusion.43, bf16[768,1152]{1,0:T(8,128)(2,1)S(1)} %copy-done, bf16[256,1152]{1,0:T(8,128)(2,1)S(1)} %collective-permute-done.16, ...), kind=kOutput, calls=%fused_computation.34 | convolution fusion | flops 1833959424 | bytes 15138816 | tf_op jit(solution)/shard_map/dot_general | solution.py:179
  131.9 3.5 convolution_convert_fusion.3
  138.5 5.2 %convolution_convert_fusion.1 = bf16[1152,1536]{1,0:T(8,128)(2,1)S(1)} fusion(bf16[1024,768]{1,0:T(8,128)(2,1)S(1)} %get-tuple-element.38, bf16[1024,768]{1,0:T(8,128)(2,1)S(1)} %get-tuple-element.39, bf16[256,1152]{1,0:T(8,128)(2,1)S(1)} %collective-permute-done.10, bf16[256,1152]{1,0:T(8,128)(2,1)} %collective-permute-done.9, ...), kind=kOutput, calls=%fused_computation.13 | convolution fusion | flops 3641376768 | bytes 9043968 | tf_op jit(solution)/shard_map/dot_general | solution.py:183
  147.3 10.3 %collective-permute-done.44 = bf16[384,1152]{1,0:T(8,128)(2,1)S(1)} collective-permute-done((bf16[384,1152]{1,0:T(8,128)(2,1)S(1)}, bf16[384,1152]{1,0:T(8,128)(2,1)S(1)}, u32[]{:S(2)}, u32[]{:S(2)}) %collective-permute-start.44) | collective-permute-done | bytes 884768 | tf_op jit(solution)/shard_map/ppermute | solution.py:117
  162.3 11.2 %collective-permute-done.13 = bf16[256,1152]{1,0:T(8,128)(2,1)S(1)} collective-permute-done((bf16[256,1152]{1,0:T(8,128)(2,1)S(1)}, bf16[256,1152]{1,0:T(8,128)(2,1)S(1)}, u32[]{:S(2)}, u32[]{:S(2)}) %collective-permute-start.13) | collective-permute-done | bytes 589856 | tf_op jit(solution)/shard_map/ppermute | solution.py:117
  175.8 5.6 %collective-permute-done.45 = bf16[192,1152]{1,0:T(8,128)(2,1)S(1)} collective-permute-done((bf16[192,1152]{1,0:T(8,128)(2,1)S(1)}, bf16[192,1152]{1,0:T(8,128)(2,1)S(1)}, u32[]{:S(2)}, u32[]{:S(2)}) %collective-permute-start.45) | collective-permute-done | bytes 442400 | tf_op jit(solution)/shard_map/ppermute | solution.py:117
  183.9 5.5 %collective-permute-done.46 = bf16[96,1152]{1,0:T(8,128)(2,1)S(1)} collective-permute-done((bf16[96,1152]{1,0:T(8,128)(2,1)S(1)}, bf16[96,1152]{1,0:T(8,128)(2,1)S(1)}, u32[]{:S(2)}, u32[]{:S(2)}) %collective-permute-start.46) | collective-permute-done | bytes 221216 | tf_op jit(solution)/shard_map/ppermute | solution.py:117
  194.0 3.3 collective-permute-done.21
  199.0 2.9 collective-permute-start.39
  201.8 18.4 %collective-permute-done.48 = bf16[192,1152]{1,0:T(8,128)(2,1)S(1)} collective-permute-done((bf16[192,1152]{1,0:T(8,128)(2,1)S(1)}, bf16[192,1152]{1,0:T(8,128)(2,1)S(1)}, u32[]{:S(2)}, u32[]{:S(2)}) %collective-permute-start.48) | collective-permute-done | bytes 442400 | tf_op jit(solution)/shard_map/ppermute | solution.py:117
  224.0 3.6 fusion.23
  227.6 7.6 %multiply_reduce_fusion = (f32[4,1024]{1,0:T(4,128)S(1)}, f32[4,1024,1024]{1,2,0:T(8,128)}) fusion(f32[4,1024,1024]{1,2,0:T(8,128)S(1)} %bitcast.74, f32[4,1024]{1,0:T(4,128)S(1)} %log_add_fusion, bf16[1024,4,72]{0,2,1:T(8,128)(2,1)S(1)} %bitcast.90, bf16[1024,4,72]{0,2,1:T(8,128)(2,1)S(1)} %bitcast.92), kind=kOutput, calls=%fused_computation.1 | convolution fusion | flops 616558592 | bytes 34766848 | tf_op jit(solution)/shard_map/qhd,khd->hqk/dot_general | solution.py:100
  235.2 11.1 %multiply_convert_fusion = bf16[4,1024,1024]{1,2,0:T(8,128)(2,1)} fusion(f32[4,1024,1024]{1,2,0:T(8,128)} %get-tuple-element.100, f32[4,1024,1024]{1,2,0:T(8,128)S(1)} %bitcast.74, f32[4,1024]{1,0:T(4,128)S(1)} %get-tuple-element.99, f32[4,1024]{1,0:T(4,128)S(1)} %log_add_fusion), kind=kLoop, calls=%fused_computation | loop fusion | flops 16777216 | bytes 41975808 | tf_op jit(solution)/shard_map/convert_element_type | solution.py:102
  246.5 6.2 %fusion.21 = f32[1024,4,72]{0,2,1:T(8,128)S(1)} fusion(bf16[4,1024,1024]{1,2,0:T(8,128)(2,1)} %multiply_convert_fusion, bf16[1024,4,18]{0,2,1:T(8,128)(2,1)S(1)} %copy-done.49, bf16[1024,4,18]{0,2,1:T(8,128)(2,1)S(1)} %copy-done.51, bf16[1024,4,18]{0,2,1:T(8,128)(2,1)S(1)} %copy-done.47, bf16[1024,4,18]{0,2,1:T(8,128)(2,1)S(1)} %copy-done.45), kind=kOutput, calls=%fused_computation.76 | convolution fusion | flops 606633984 | bytes 10158080 | tf_op jit(solution)/shard_map/hqk,qhd->khd/dot_general | solution.py:109
  284.9 4.2 collective-permute-done.33
  289.9 6.1 %collective-permute-done.34 = bf16[36,1152]{1,0:T(8,128)(2,1)S(1)} collective-permute-done((bf16[36,1152]{1,0:T(8,128)(2,1)S(1)}, bf16[36,1152]{1,0:T(8,128)(2,1)S(1)}, u32[]{:S(2)}, u32[]{:S(2)}) %collective-permute-start.34) | collective-permute-done | bytes 82976 | tf_op jit(solution)/shard_map/ppermute | solution.py:117
  296.0 3.0 collective-permute-start.35
  299.9 20.6 %collective-permute-done.35 = bf16[36,1152]{1,0:T(8,128)(2,1)S(1)} collective-permute-done((bf16[36,1152]{1,0:T(8,128)(2,1)S(1)}, bf16[36,1152]{1,0:T(8,128)(2,1)S(1)}, u32[]{:S(2)}, u32[]{:S(2)}) %collective-permute-start.35) | collective-permute-done | bytes 82976 | tf_op jit(solution)/shard_map/ppermute | solution.py:117
  322.1 2.9 collective-permute-start.41
  325.0 4.1 fusion.16
  336.1 3.0 collective-permute-done.37
  352.1 2.6 fusion.32
  354.7 14.5 %collective-permute-done.56 = bf16[4,7056]{1,0:T(4,128)(2,1)S(1)} collective-permute-done((bf16[4,7056]{1,0:T(4,128)(2,1)S(1)}, bf16[4,7056]{1,0:T(4,128)(2,1)S(1)}, u32[]{:S(2)}, u32[]{:S(2)}) %collective-permute-start.56) | collective-permute-done | bytes 56480 | tf_op jit(solution)/shard_map/ppermute | solution.py:117
  369.2 2.6 collective-permute-start.57
  374.2 5.3 %collective-permute-done.57 = bf16[8,7056]{1,0:T(8,128)(2,1)S(1)} collective-permute-done((bf16[8,7056]{1,0:T(8,128)(2,1)S(1)}, bf16[8,7056]{1,0:T(8,128)(2,1)S(1)}, u32[]{:S(2)}, u32[]{:S(2)}) %collective-permute-start.57) | collective-permute-done | bytes 112928 | tf_op jit(solution)/shard_map/ppermute | solution.py:117
  380.2 14.5 %collective-permute-done.28 = bf16[144,864]{0,1:T(8,128)(2,1)S(1)} collective-permute-done((bf16[144,864]{0,1:T(8,128)(2,1)S(1)}, bf16[144,864]{0,1:T(8,128)(2,1)S(1)}, u32[]{:S(2)}, u32[]{:S(2)}) %collective-permute-start.28) | collective-permute-done | bytes 248864 | tf_op jit(solution)/shard_map/ppermute | solution.py:117
  395.2 21.5 %collective-permute-done.29 = bf16[144,864]{0,1:T(8,128)(2,1)S(1)} collective-permute-done((bf16[144,864]{0,1:T(8,128)(2,1)S(1)}, bf16[144,864]{0,1:T(8,128)(2,1)S(1)}, u32[]{:S(2)}, u32[]{:S(2)}) %collective-permute-start.29) | collective-permute-done | bytes 248864 | tf_op jit(solution)/shard_map/ppermute | solution.py:117
  418.2 3.4 fusion.44
  421.5 9.5 %collective-permute-done.30 = bf16[288,864]{1,0:T(8,128)(2,1)S(1)} collective-permute-done((bf16[288,864]{1,0:T(8,128)(2,1)S(1)}, bf16[288,864]{1,0:T(8,128)(2,1)S(1)}, u32[]{:S(2)}, u32[]{:S(2)}) %collective-permute-start.30) | collective-permute-done | bytes 497696 | tf_op jit(solution)/shard_map/ppermute | solution.py:117
  441.3 4.5 fusion.46
  445.8 14.5 %collective-permute-done.31 = bf16[576,864]{1,0:T(8,128)(2,1)} collective-permute-done((bf16[576,864]{1,0:T(8,128)(2,1)}, bf16[576,864]{1,0:T(8,128)(2,1)}, u32[]{:S(2)}, u32[]{:S(2)}) %collective-permute-start.31) | collective-permute-done | bytes 995360 | tf_op jit(solution)/shard_map/ppermute | solution.py:117
  462.6 2.9 fusion.15
  467.5 28.7 %collective-permute-done.43 = bf16[576,1536]{1,0:T(8,128)(2,1)} collective-permute-done((bf16[576,1536]{1,0:T(8,128)(2,1)S(1)}, bf16[576,1536]{1,0:T(8,128)(2,1)}, u32[]{:S(2)}, u32[]{:S(2)}) %collective-permute-start.43) | collective-permute-done | bytes 1769504 | tf_op jit(solution)/shard_map/ppermute | solution.py:117
  496.2 2.7 fusion.10
  498.9 3.4 fusion.110
  (504 shorter events, 149.9 us)
Async XLA Ops:
  0.7 19.9 %collective-permute-start.2 = (bf16[256,1152]{1,0:T(8,128)(2,1)}, bf16[256,1152]{1,0:T(8,128)(2,1)S(1)}, u32[]{:S(2)}, u32[]{:S(2)}) collective-permute-start(bf16[256,1152]{1,0:T(8,128)(2,1)} %param.17), channel_id=1, source_target_pairs={{0,1},{1,0},{2,3},{3,2},{4,5},{5,4},{6,7},{7,6},{8,9},{9,8},{10,11... | collective-permute-start | bytes 1769480 | tf_op jit(solution)/shard_map/ppermute | solution.py:117
  1.2 17.0 %collective-permute-start.3 = (bf16[256,1152]{1,0:T(8,128)(2,1)}, bf16[256,1152]{1,0:T(8,128)(2,1)S(1)}, u32[]{:S(2)}, u32[]{:S(2)}) collective-permute-start(bf16[256,1152]{1,0:T(8,128)(2,1)} %param.17), channel_id=1, source_target_pairs={{0,2},{1,3},{2,0},{3,1},{4,6},{5,7},{6,4},{7,5},{8,10},{9,11},{10,... | collective-permute-start | bytes 1769480 | tf_op jit(solution)/shard_map/ppermute | solution.py:117
  56.9 12.5 %collective-permute-start.50 = (s32[4,2]{0,1:T(2,128)}, s32[4,2]{0,1:T(2,128)S(1)}, u32[]{:S(2)}, u32[]{:S(2)}) collective-permute-start(s32[4,2]{0,1:T(2,128)} %pad_add_fusion.6), channel_id=1, source_target_pairs={{0,16},{4,20},{8,24},{12,28},{16,0},{20,4},{24,8},{28,12},{1,17},{... | collective-permute-start | bytes 104 | tf_op jit(solution)/shard_map/ppermute | solution.py:117
  62.5 10.0 %collective-permute-start.5 = (bf16[256,1152]{1,0:T(8,128)(2,1)}, bf16[256,1152]{1,0:T(8,128)(2,1)S(1)}, u32[]{:S(2)}, u32[]{:S(2)}) collective-permute-start(bf16[256,1152]{1,0:T(8,128)(2,1)} %slice.214), channel_id=1, source_target_pairs={{0,1},{1,0},{2,3},{3,2},{4,5},{5,4},{6,7},{7,6},{8,9},{9,8},{10,11... | collective-permute-start | bytes 1769480 | tf_op jit(solution)/shard_map/ppermute | solution.py:117
  63.7 15.8 %collective-permute-start.7 = (bf16[256,1152]{1,0:T(8,128)(2,1)}, bf16[256,1152]{1,0:T(8,128)(2,1)S(1)}, u32[]{:S(2)}, u32[]{:S(2)}) collective-permute-start(bf16[256,1152]{1,0:T(8,128)(2,1)} %add_convert_fusion.10), channel_id=1, source_target_pairs={{0,2},{1,3},{2,0},{3,1},{4,6},{5,7},{6,4},{7,5},{8,10},{9,11},{10,... | collective-permute-start | bytes 1769480 | tf_op jit(solution)/shard_map/ppermute | solution.py:117
  69.5 17.2 %collective-permute-start.51 = (s32[8,2]{0,1:T(2,128)S(1)}, s32[8,2]{0,1:T(2,128)S(1)}, u32[]{:S(2)}, u32[]{:S(2)}) collective-permute-start(s32[8,2]{0,1:T(2,128)S(1)} %pad_add_fusion.7), channel_id=1, source_target_pairs={{0,8},{4,12},{8,0},{12,4},{16,24},{20,28},{24,16},{28,20},{1,9},{5... | collective-permute-start | bytes 200 | tf_op jit(solution)/shard_map/ppermute | solution.py:117
  83.7 16.6 %collective-permute-start.9 = (bf16[256,1152]{1,0:T(8,128)(2,1)}, bf16[256,1152]{1,0:T(8,128)(2,1)}, u32[]{:S(2)}, u32[]{:S(2)}) collective-permute-start(bf16[256,1152]{1,0:T(8,128)(2,1)} %add_convert_fusion.9), channel_id=1, source_target_pairs={{0,2},{1,3},{2,0},{3,1},{4,6},{5,7},{6,4},{7,5},{8,10},{9,11},{10,... | collective-permute-start | bytes 1769480 | tf_op jit(solution)/shard_map/ppermute | solution.py:117
  86.1 25.3 %collective-permute-start.15 = (bf16[256,1152]{1,0:T(8,128)(2,1)}, bf16[256,1152]{1,0:T(8,128)(2,1)}, u32[]{:S(2)}, u32[]{:S(2)}) collective-permute-start(bf16[256,1152]{1,0:T(8,128)(2,1)} %fusion.27), channel_id=1, source_target_pairs={{0,2},{1,3},{2,0},{3,1},{4,6},{5,7},{6,4},{7,5},{8,10},{9,11},{10,... | collective-permute-start | bytes 1769480 | tf_op jit(solution)/shard_map/ppermute | solution.py:117
  92.0 20.2 %collective-permute-start.8 = (bf16[256,1152]{1,0:T(8,128)(2,1)}, bf16[256,1152]{1,0:T(8,128)(2,1)S(1)}, u32[]{:S(2)}, u32[]{:S(2)}) collective-permute-start(bf16[256,1152]{1,0:T(8,128)(2,1)} %add_convert_fusion.9), channel_id=1, source_target_pairs={{0,1},{1,0},{2,3},{3,2},{4,5},{5,4},{6,7},{7,6},{8,9},{9,8},{10,11... | collective-permute-start | bytes 1769480 | tf_op jit(solution)/shard_map/ppermute | solution.py:117
  100.3 11.9 %collective-permute-start.10 = (bf16[256,1152]{1,0:T(8,128)(2,1)}, bf16[256,1152]{1,0:T(8,128)(2,1)S(1)}, u32[]{:S(2)}, u32[]{:S(2)}) collective-permute-start(bf16[256,1152]{1,0:T(8,128)(2,1)} %collective-permute-done.9), channel_id=1, source_target_pairs={{0,1},{1,0},{2,3},{3,2},{4,5},{5,4},{6,7},{7,6},{8,9},{9,8},{10,11... | collective-permute-start | bytes 1769480 | tf_op jit(solution)/shard_map/ppermute | solution.py:117
  102.3 16.4 %collective-permute-start.14 = (bf16[256,1152]{1,0:T(8,128)(2,1)}, bf16[256,1152]{1,0:T(8,128)(2,1)S(1)}, u32[]{:S(2)}, u32[]{:S(2)}) collective-permute-start(bf16[256,1152]{1,0:T(8,128)(2,1)} %fusion.27), channel_id=1, source_target_pairs={{0,1},{1,0},{2,3},{3,2},{4,5},{5,4},{6,7},{7,6},{8,9},{9,8},{10,11... | collective-permute-start | bytes 1769480 | tf_op jit(solution)/shard_map/ppermute | solution.py:117
  111.4 7.4 %collective-permute-start.16 = (bf16[256,1152]{1,0:T(8,128)(2,1)}, bf16[256,1152]{1,0:T(8,128)(2,1)S(1)}, u32[]{:S(2)}, u32[]{:S(2)}) collective-permute-start(bf16[256,1152]{1,0:T(8,128)(2,1)} %collective-permute-done.15), channel_id=1, source_target_pairs={{0,1},{1,0},{2,3},{3,2},{4,5},{5,4},{6,7},{7,6},{8,9},{9,8},{10,11... | collective-permute-start | bytes 1769480 | tf_op jit(solution)/shard_map/ppermute | solution.py:117
  135.5 22.1 %collective-permute-start.44 = (bf16[384,1152]{1,0:T(8,128)(2,1)S(1)}, bf16[384,1152]{1,0:T(8,128)(2,1)S(1)}, u32[]{:S(2)}, u32[]{:S(2)}) collective-permute-start(bf16[384,1152]{1,0:T(8,128)(2,1)S(1)} %constant_dynamic-slice_fusion.2), channel_id=1, source_target_pairs={{0,8},{4,12},{8,0},{12,4},{16,24},{20,28},{24,16},{28,20},{1,9},{5... | collective-permute-start | bytes 2654216 | tf_op jit(solution)/shard_map/ppermute | solution.py:117
  137.3 22.2 %collective-permute-start.17 = (bf16[256,1152]{1,0:T(8,128)(2,1)S(1)}, bf16[256,1152]{1,0:T(8,128)(2,1)S(1)}, u32[]{:S(2)}, u32[]{:S(2)}) collective-permute-start(bf16[256,1152]{1,0:T(8,128)(2,1)S(1)} %slice.227), channel_id=1, source_target_pairs={{0,1},{1,0},{2,3},{3,2},{4,5},{5,4},{6,7},{7,6},{8,9},{9,8},{10,11... | collective-permute-start | bytes 1769480 | tf_op jit(solution)/shard_map/ppermute | solution.py:117
  137.9 7.7 %collective-permute-start.12 = (bf16[256,1152]{1,0:T(8,128)(2,1)S(1)}, bf16[256,1152]{1,0:T(8,128)(2,1)S(1)}, u32[]{:S(2)}, u32[]{:S(2)}) collective-permute-start(bf16[256,1152]{1,0:T(8,128)(2,1)S(1)} %slice.223), channel_id=1, source_target_pairs={{0,1},{1,0},{2,3},{3,2},{4,5},{5,4},{6,7},{7,6},{8,9},{9,8},{10,11... | collective-permute-start | bytes 1769480 | tf_op jit(solution)/shard_map/ppermute | solution.py:117
  138.2 24.0 %collective-permute-start.11 = (bf16[256,1152]{1,0:T(8,128)(2,1)S(1)}, bf16[256,1152]{1,0:T(8,128)(2,1)S(1)}, u32[]{:S(2)}, u32[]{:S(2)}) collective-permute-start(bf16[256,1152]{1,0:T(8,128)(2,1)S(1)} %slice.220), channel_id=1, source_target_pairs={{0,1},{1,0},{2,3},{3,2},{4,5},{5,4},{6,7},{7,6},{8,9},{9,8},{10,11... | collective-permute-start | bytes 1769480 | tf_op jit(solution)/shard_map/ppermute | solution.py:117
  143.8 53.6 %collective-permute-start.38 = (bf16[576,1536]{1,0:T(8,128)(2,1)S(1)}, bf16[576,1536]{1,0:T(8,128)(2,1)S(1)}, u32[]{:S(2)}, u32[]{:S(2)}) collective-permute-start(bf16[576,1536]{1,0:T(8,128)(2,1)S(1)} %constant_dynamic-slice_fusion.5), channel_id=1, source_target_pairs={{0,4},{4,0},{8,12},{12,8},{16,20},{20,16},{24,28},{28,24},{1,5},{5... | collective-permute-start | bytes 5308424 | tf_op jit(solution)/shard_map/ppermute | solution.py:117
  145.6 16.1 %collective-permute-start.19 = (bf16[256,1152]{1,0:T(8,128)(2,1)S(1)}, bf16[256,1152]{1,0:T(8,128)(2,1)S(1)}, u32[]{:S(2)}, u32[]{:S(2)}) collective-permute-start(bf16[256,1152]{1,0:T(8,128)(2,1)S(1)} %add_convert_fusion.6), channel_id=1, source_target_pairs={{0,2},{1,3},{2,0},{3,1},{4,6},{5,7},{6,4},{7,5},{8,10},{9,11},{10,... | collective-permute-start | bytes 1769480 | tf_op jit(solution)/shard_map/ppermute | solution.py:117
  157.7 15.8 %collective-permute-start.13 = (bf16[256,1152]{1,0:T(8,128)(2,1)S(1)}, bf16[256,1152]{1,0:T(8,128)(2,1)S(1)}, u32[]{:S(2)}, u32[]{:S(2)}) collective-permute-start(bf16[256,1152]{1,0:T(8,128)(2,1)S(1)} %add_convert_fusion.8), channel_id=1, source_target_pairs={{0,2},{1,3},{2,0},{3,1},{4,6},{5,7},{6,4},{7,5},{8,10},{9,11},{10,... | collective-permute-start | bytes 1769480 | tf_op jit(solution)/shard_map/ppermute | solution.py:117
  159.5 22.0 %collective-permute-start.45 = (bf16[192,1152]{1,0:T(8,128)(2,1)S(1)}, bf16[192,1152]{1,0:T(8,128)(2,1)S(1)}, u32[]{:S(2)}, u32[]{:S(2)}) collective-permute-start(bf16[192,1152]{1,0:T(8,128)(2,1)S(1)} %constant_dynamic-slice_fusion.1), channel_id=1, source_target_pairs={{0,16},{4,20},{8,24},{12,28},{16,0},{20,4},{24,8},{28,12},{1,17},{... | collective-permute-start | bytes 1327112 | tf_op jit(solution)/shard_map/ppermute | solution.py:117
  181.6 7.7 %collective-permute-start.46 = (bf16[96,1152]{1,0:T(8,128)(2,1)S(1)}, bf16[96,1152]{1,0:T(8,128)(2,1)S(1)}, u32[]{:S(2)}, u32[]{:S(2)}) collective-permute-start(bf16[96,1152]{1,0:T(8,128)(2,1)S(1)} %constant_dynamic-slice_fusion), channel_id=1, source_target_pairs={{0,4},{4,0},{8,12},{12,8},{16,20},{20,16},{24,28},{28,24},{1,5},{5... | collective-permute-start | bytes 663560 | tf_op jit(solution)/shard_map/ppermute | solution.py:117
  183.3 14.0 %collective-permute-start.21 = (bf16[256,1152]{1,0:T(8,128)(2,1)S(1)}, bf16[256,1152]{1,0:T(8,128)(2,1)S(1)}, u32[]{:S(2)}, u32[]{:S(2)}) collective-permute-start(bf16[256,1152]{1,0:T(8,128)(2,1)S(1)} %multiply_convert_fusion.3), channel_id=1, source_target_pairs={{0,2},{1,3},{2,0},{3,1},{4,6},{5,7},{6,4},{7,5},{8,10},{9,11},{10,... | collective-permute-start | bytes 1769480 | tf_op jit(solution)/shard_map/ppermute | solution.py:117
  189.4 7.8 %collective-permute-start.47 = (bf16[96,1152]{1,0:T(8,128)(2,1)S(1)}, bf16[96,1152]{1,0:T(8,128)(2,1)S(1)}, u32[]{:S(2)}, u32[]{:S(2)}) collective-permute-start(bf16[96,1152]{1,0:T(8,128)(2,1)S(1)} %add_convert_fusion.15), channel_id=1, source_target_pairs={{0,4},{4,0},{8,12},{12,8},{16,20},{20,16},{24,28},{28,24},{1,5},{5... | collective-permute-start | bytes 663560 | tf_op jit(solution)/shard_map/ppermute | solution.py:117
  191.6 29.8 %collective-permute-start.20 = (bf16[256,1152]{1,0:T(8,128)(2,1)S(1)}, bf16[256,1152]{1,0:T(8,128)(2,1)S(1)}, u32[]{:S(2)}, u32[]{:S(2)}) collective-permute-start(bf16[256,1152]{1,0:T(8,128)(2,1)S(1)} %multiply_convert_fusion.3), channel_id=1, source_target_pairs={{0,1},{1,0},{2,3},{3,2},{4,5},{5,4},{6,7},{7,6},{8,9},{9,8},{10,11... | collective-permute-start | bytes 1769480 | tf_op jit(solution)/shard_map/ppermute | solution.py:117
  197.3 24.1 %collective-permute-start.22 = (bf16[256,1152]{1,0:T(8,128)(2,1)S(1)}, bf16[256,1152]{1,0:T(8,128)(2,1)S(1)}, u32[]{:S(2)}, u32[]{:S(2)}) collective-permute-start(bf16[256,1152]{1,0:T(8,128)(2,1)S(1)} %collective-permute-done.21), channel_id=1, source_target_pairs={{0,1},{1,0},{2,3},{3,2},{4,5},{5,4},{6,7},{7,6},{8,9},{9,8},{10,11... | collective-permute-start | bytes 1769480 | tf_op jit(solution)/shard_map/ppermute | solution.py:117
  197.4 22.8 %collective-permute-start.48 = (bf16[192,1152]{1,0:T(8,128)(2,1)S(1)}, bf16[192,1152]{1,0:T(8,128)(2,1)S(1)}, u32[]{:S(2)}, u32[]{:S(2)}) collective-permute-start(bf16[192,1152]{1,0:T(8,128)(2,1)S(1)} %maximum_select_fusion.9), channel_id=1, source_target_pairs={{0,16},{4,20},{8,24},{12,28},{16,0},{20,4},{24,8},{28,12},{1,17},{... | collective-permute-start | bytes 1327112 | tf_op jit(solution)/shard_map/ppermute | solution.py:117
  199.0 83.9 %collective-permute-start.39 = (bf16[288,1536]{1,0:T(8,128)(2,1)}, bf16[288,1536]{1,0:T(8,128)(2,1)}, u32[]{:S(2)}, u32[]{:S(2)}) collective-permute-start(bf16[288,1536]{1,0:T(8,128)(2,1)} %constant_dynamic-slice_fusion.4), channel_id=1, source_target_pairs={{0,8},{4,12},{8,0},{12,4},{16,24},{20,28},{24,16},{28,20},{1,9},{5... | collective-permute-start | bytes 2654216 | tf_op jit(solution)/shard_map/ppermute | solution.py:117
  221.4 100.7 %collective-permute-start.49 = (bf16[384,1152]{1,0:T(8,128)(2,1)}, bf16[384,1152]{1,0:T(8,128)(2,1)}, u32[]{:S(2)}, u32[]{:S(2)}) collective-permute-start(bf16[384,1152]{1,0:T(8,128)(2,1)} %maximum_select_fusion.6), channel_id=1, source_target_pairs={{0,8},{4,12},{8,0},{12,4},{16,24},{20,28},{24,16},{28,20},{1,9},{5... | collective-permute-start | bytes 2654216 | tf_op jit(solution)/shard_map/ppermute | solution.py:117
  268.6 12.5 %collective-permute-start.32 = (bf16[144,1152]{1,0:T(8,128)(2,1)}, bf16[144,1152]{1,0:T(8,128)(2,1)}, u32[]{:S(2)}, u32[]{:S(2)}) collective-permute-start(bf16[144,1152]{1,0:T(8,128)(2,1)} %constant_dynamic-slice_fusion.8), channel_id=1, source_target_pairs={{0,4},{4,0},{8,12},{12,8},{16,20},{20,16},{24,28},{28,24},{1,5},{5... | collective-permute-start | bytes 995336 | tf_op jit(solution)/shard_map/ppermute | solution.py:117
  276.6 54.0 %collective-permute-start.26 = (bf16[576,864]{1,0:T(8,128)(2,1)}, bf16[576,864]{1,0:T(8,128)(2,1)}, u32[]{:S(2)}, u32[]{:S(2)}) collective-permute-start(bf16[576,864]{1,0:T(8,128)(2,1)} %copy.59), channel_id=1, source_target_pairs={{0,4},{4,0},{8,12},{12,8},{16,20},{20,16},{24,28},{28,24},{1,5},{5... | collective-permute-start | bytes 2985992 | tf_op jit(solution)/shard_map/ppermute | solution.py:117
  281.2 60.4 %collective-permute-start.23 = (bf16[256,1152]{1,0:T(8,128)(2,1)}, bf16[256,1152]{1,0:T(8,128)(2,1)}, u32[]{:S(2)}, u32[]{:S(2)}) collective-permute-start(bf16[256,1152]{1,0:T(8,128)(2,1)} %slice.234), channel_id=1, source_target_pairs={{0,1},{1,0},{2,3},{3,2},{4,5},{5,4},{6,7},{7,6},{8,9},{9,8},{10,11... | collective-permute-start | bytes 1769480 | tf_op jit(solution)/shard_map/ppermute | solution.py:117
  281.2 14.8 %collective-permute-start.24 = (bf16[256,1152]{1,0:T(8,128)(2,1)S(1)}, bf16[256,1152]{1,0:T(8,128)(2,1)S(1)}, u32[]{:S(2)}, u32[]{:S(2)}) collective-permute-start(bf16[256,1152]{1,0:T(8,128)(2,1)S(1)} %slice.237), channel_id=1, source_target_pairs={{0,1},{1,0},{2,3},{3,2},{4,5},{5,4},{6,7},{7,6},{8,9},{9,8},{10,11... | collective-permute-start | bytes 1769480 | tf_op jit(solution)/shard_map/ppermute | solution.py:117
  295.9 25.2 %collective-permute-start.40 = (bf16[144,1536]{1,0:T(8,128)(2,1)S(1)}, bf16[144,1536]{1,0:T(8,128)(2,1)S(1)}, u32[]{:S(2)}, u32[]{:S(2)}) collective-permute-start(bf16[144,1536]{1,0:T(8,128)(2,1)S(1)} %constant_dynamic-slice_fusion.3), channel_id=1, source_target_pairs={{0,16},{4,20},{8,24},{12,28},{16,0},{20,4},{24,8},{28,12},{1,17},{... | collective-permute-start | bytes 1327112 | tf_op jit(solution)/shard_map/ppermute | solution.py:117
  296.0 24.5 %collective-permute-start.35 = (bf16[36,1152]{1,0:T(8,128)(2,1)S(1)}, bf16[36,1152]{1,0:T(8,128)(2,1)S(1)}, u32[]{:S(2)}, u32[]{:S(2)}) collective-permute-start(bf16[36,1152]{1,0:T(8,128)(2,1)S(1)} %add_convert_fusion.21), channel_id=1, source_target_pairs={{0,16},{4,20},{8,24},{12,28},{16,0},{20,4},{24,8},{28,12},{1,17},{... | collective-permute-start | bytes 248840 | tf_op jit(solution)/shard_map/ppermute | solution.py:117
  320.5 21.1 %collective-permute-start.25 = (bf16[256,1152]{1,0:T(8,128)(2,1)}, bf16[256,1152]{1,0:T(8,128)(2,1)}, u32[]{:S(2)}, u32[]{:S(2)}) collective-permute-start(bf16[256,1152]{1,0:T(8,128)(2,1)} %add_convert_fusion.5), channel_id=1, source_target_pairs={{0,2},{1,3},{2,0},{3,1},{4,6},{5,7},{6,4},{7,5},{8,10},{9,11},{10,... | collective-permute-start | bytes 1769480 | tf_op jit(solution)/shard_map/ppermute | solution.py:117
  321.1 8.1 %collective-permute-start.36 = (bf16[72,1152]{1,0:T(8,128)(2,1)S(1)}, bf16[72,1152]{1,0:T(8,128)(2,1)S(1)}, u32[]{:S(2)}, u32[]{:S(2)}) collective-permute-start(bf16[72,1152]{1,0:T(8,128)(2,1)S(1)} %maximum_select_fusion.11), channel_id=1, source_target_pairs={{0,8},{4,12},{8,0},{12,4},{16,24},{20,28},{24,16},{28,20},{1,9},{5... | collective-permute-start | bytes 497672 | tf_op jit(solution)/shard_map/ppermute | solution.py:117
  322.1 23.2 %collective-permute-start.41 = (bf16[144,1536]{1,0:T(8,128)(2,1)}, bf16[144,1536]{1,0:T(8,128)(2,1)}, u32[]{:S(2)}, u32[]{:S(2)}) collective-permute-start(bf16[144,1536]{1,0:T(8,128)(2,1)} %add_convert_fusion.12), channel_id=1, source_target_pairs={{0,16},{4,20},{8,24},{12,28},{16,0},{20,4},{24,8},{28,12},{1,17},{... | collective-permute-start | bytes 1327112 | tf_op jit(solution)/shard_map/ppermute | solution.py:117
  330.0 9.1 %collective-permute-start.37 = (bf16[144,1152]{1,0:T(8,128)(2,1)}, bf16[144,1152]{1,0:T(8,128)(2,1)}, u32[]{:S(2)}, u32[]{:S(2)}) collective-permute-start(bf16[144,1152]{1,0:T(8,128)(2,1)} %maximum_select_fusion.10), channel_id=1, source_target_pairs={{0,4},{4,0},{8,12},{12,8},{16,20},{20,16},{24,28},{28,24},{1,5},{5... | collective-permute-start | bytes 995336 | tf_op jit(solution)/shard_map/ppermute | solution.py:117
  336.0 35.8 %collective-permute-start.27 = (bf16[288,864]{1,0:T(8,128)(2,1)}, bf16[288,864]{1,0:T(8,128)(2,1)S(1)}, u32[]{:S(2)}, u32[]{:S(2)}) collective-permute-start(bf16[288,864]{1,0:T(8,128)(2,1)} %copy.61), channel_id=1, source_target_pairs={{0,8},{4,12},{8,0},{12,4},{16,24},{20,28},{24,16},{28,20},{1,9},{5... | collective-permute-start | bytes 1493000 | tf_op jit(solution)/shard_map/ppermute | solution.py:117
  347.8 87.8 %collective-permute-start.42 = (bf16[288,1536]{1,0:T(8,128)(2,1)}, bf16[288,1536]{1,0:T(8,128)(2,1)}, u32[]{:S(2)}, u32[]{:S(2)}) collective-permute-start(bf16[288,1536]{1,0:T(8,128)(2,1)} %maximum_select_fusion.5), channel_id=1, source_target_pairs={{0,8},{4,12},{8,0},{12,4},{16,24},{20,28},{24,16},{28,20},{1,9},{5... | collective-permute-start | bytes 2654216 | tf_op jit(solution)/shard_map/ppermute | solution.py:117
  350.0 19.2 %collective-permute-start.56 = (bf16[4,7056]{1,0:T(4,128)(2,1)S(1)}, bf16[4,7056]{1,0:T(4,128)(2,1)S(1)}, u32[]{:S(2)}, u32[]{:S(2)}) collective-permute-start(bf16[4,7056]{1,0:T(4,128)(2,1)S(1)} %pad_maximum_fusion.19), channel_id=1, source_target_pairs={{0,16},{4,20},{8,24},{12,28},{16,0},{20,4},{24,8},{28,12},{1,17},{... | collective-permute-start | bytes 169352 | tf_op jit(solution)/shard_map/ppermute | solution.py:117
  369.2 10.3 %collective-permute-start.57 = (bf16[8,7056]{1,0:T(8,128)(2,1)S(1)}, bf16[8,7056]{1,0:T(8,128)(2,1)S(1)}, u32[]{:S(2)}, u32[]{:S(2)}) collective-permute-start(bf16[8,7056]{1,0:T(8,128)(2,1)S(1)} %pad_maximum_fusion.18), channel_id=1, source_target_pairs={{0,8},{4,12},{8,0},{12,4},{16,24},{20,28},{24,16},{28,20},{1,9},{5... | collective-permute-start | bytes 338696 | tf_op jit(solution)/shard_map/ppermute | solution.py:117
  372.8 22.0 %collective-permute-start.28 = (bf16[144,864]{0,1:T(8,128)(2,1)S(1)}, bf16[144,864]{0,1:T(8,128)(2,1)S(1)}, u32[]{:S(2)}, u32[]{:S(2)}) collective-permute-start(bf16[144,864]{0,1:T(8,128)(2,1)S(1)} %constant_dynamic-slice_fusion.9), channel_id=1, source_target_pairs={{0,16},{4,20},{8,24},{12,28},{16,0},{20,4},{24,8},{28,12},{1,17},{... | collective-permute-start | bytes 746504 | tf_op jit(solution)/shard_map/ppermute | solution.py:117
  379.6 15.4 %collective-permute-start.58 = (bf16[16,7056]{1,0:T(8,128)(2,1)S(1)}, bf16[16,7056]{1,0:T(8,128)(2,1)S(1)}, u32[]{:S(2)}, u32[]{:S(2)}) collective-permute-start(bf16[16,7056]{1,0:T(8,128)(2,1)S(1)} %pad_maximum_fusion.16), channel_id=1, source_target_pairs={{0,4},{4,0},{8,12},{12,8},{16,20},{20,16},{24,28},{28,24},{1,5},{5... | collective-permute-start | bytes 677384 | tf_op jit(solution)/shard_map/ppermute | solution.py:117
  395.0 21.7 %collective-permute-start.29 = (bf16[144,864]{0,1:T(8,128)(2,1)S(1)}, bf16[144,864]{0,1:T(8,128)(2,1)S(1)}, u32[]{:S(2)}, u32[]{:S(2)}) collective-permute-start(bf16[144,864]{0,1:T(8,128)(2,1)S(1)} %add_convert_fusion.13), channel_id=1, source_target_pairs={{0,16},{4,20},{8,24},{12,28},{16,0},{20,4},{24,8},{28,12},{1,17},{... | collective-permute-start | bytes 746504 | tf_op jit(solution)/shard_map/ppermute | solution.py:117
  417.5 13.6 %collective-permute-start.30 = (bf16[288,864]{1,0:T(8,128)(2,1)S(1)}, bf16[288,864]{1,0:T(8,128)(2,1)S(1)}, u32[]{:S(2)}, u32[]{:S(2)}) collective-permute-start(bf16[288,864]{1,0:T(8,128)(2,1)S(1)} %copy.63), channel_id=1, source_target_pairs={{0,8},{4,12},{8,0},{12,4},{16,24},{20,28},{24,16},{28,20},{1,9},{5... | collective-permute-start | bytes 1493000 | tf_op jit(solution)/shard_map/ppermute | solution.py:117
  434.2 26.1 %collective-permute-start.31 = (bf16[576,864]{1,0:T(8,128)(2,1)}, bf16[576,864]{1,0:T(8,128)(2,1)}, u32[]{:S(2)}, u32[]{:S(2)}) collective-permute-start(bf16[576,864]{1,0:T(8,128)(2,1)} %copy.66), channel_id=1, source_target_pairs={{0,4},{4,0},{8,12},{12,8},{16,20},{20,16},{24,28},{28,24},{1,5},{5... | collective-permute-start | bytes 2985992 | tf_op jit(solution)/shard_map/ppermute | solution.py:117
  438.1 58.1 %collective-permute-start.43 = (bf16[576,1536]{1,0:T(8,128)(2,1)S(1)}, bf16[576,1536]{1,0:T(8,128)(2,1)}, u32[]{:S(2)}, u32[]{:S(2)}) collective-permute-start(bf16[576,1536]{1,0:T(8,128)(2,1)S(1)} %maximum_select_fusion.2), channel_id=1, source_target_pairs={{0,4},{4,0},{8,12},{12,8},{16,20},{20,16},{24,28},{28,24},{1,5},{5... | collective-permute-start | bytes 5308424 | tf_op jit(solution)/shard_map/ppermute | solution.py:117
  (137 other events, 1176.3 us)

commit v2 on v1

v2 whole, which is shorter than its diff:
```python
import functools
import math

import jax
import jax.numpy as jnp
from jax import lax
from jax.experimental import pallas as pl
from jax.experimental.pallas import tpu as pltpu
from jax.sharding import PartitionSpec as P

D = 1152
HEAD_DIM = 72
PAD = 128
SIDE = 16
SLOT_TOK = 256
EPSILON = 1e-06
SCORE_LOG2 = math.log2(math.e) / math.sqrt(HEAD_DIM)
INV_ROOT = 1.0 / math.sqrt(HEAD_DIM)
TOTAL_LANE = HEAD_DIM
DOT_LANE = HEAD_DIM + 1
ITEM_LANE = HEAD_DIM + 4
LOG_LANE = ITEM_LANE + 8
FAR_ITEM = 16384.0
CONTRACT_ROWS = (((0,), (0,)), ((), ()))
CONTRACT_COLS = (((1,), (1,)), ((), ()))
VMEM_LIMIT = 56 * 1024 * 1024


def sinusoid(step_ids, first_col, col_count):
    half_width = D // 2
    feature = first_col + jnp.arange(col_count, dtype=jnp.int32)
    freq_index = (feature % half_width).astype(jnp.float32)
    rates = jnp.exp(-math.log(10000.0) * freq_index / half_width)
    angles = step_ids.astype(jnp.float32)[:, None] * rates[None, :]
    return jnp.where(feature[None, :] < half_width, jnp.cos(angles), jnp.sin(angles))


def grid_positions(slot_ids):
    slot_count = slot_ids.shape[0]
    slot_order = jnp.arange(slot_count, dtype=jnp.int32)
    same_item = (slot_ids[:, None] == slot_ids[None, :]) & (slot_ids[:, None] >= 0)
    members = jnp.sum(same_item.astype(jnp.int32), axis=1)
    first_slot = jnp.min(jnp.where(same_item, slot_order[None, :], slot_count), axis=1)
    first_slot = jnp.where(members > 0, first_slot, slot_order)
    side_len = jnp.where(members > 1, 2 * SIDE, SIDE)
    within = jnp.arange(SLOT_TOK, dtype=jnp.int32)
    place_in = (slot_order - first_slot)[:, None] * SLOT_TOK + within[None, :]
    return ((place_in // side_len[:, None]).reshape(-1), (place_in % side_len[:, None]).reshape(-1))


def modulated_norm(values, shift_by, scale_by):
    normed = values * lax.rsqrt(jnp.mean(values * values, axis=-1, keepdims=True) + EPSILON)
    return normed * (1.0 + scale_by[:, None, :]) + shift_by[:, None, :]


def full_dot(left, right, dims=(((1,), (0,)), ((), ()))):
    return lax.dot_general(left, right, dims, preferred_element_type=jnp.float32)


def rotate(values, cosine, sine_front, sine_back):
    quarter = HEAD_DIM // 4
    return (
        values * cosine
        + pltpu.roll(values, PAD - quarter, 1) * sine_front
        + pltpu.roll(values, quarter, 1) * sine_back
    )


def head_inverse(lin):
    return lax.rsqrt(jnp.sum(lin * lin, axis=-1, keepdims=True) * (1.0 / HEAD_DIM) + EPSILON)


def prepare_kernel(
    x_ref, mod_ref, wq_ref, wk_ref, wv_ref, cos_ref, front_ref, back_ref, gain_ref, extra_ref,
    normed_ref, lin_ref, q_ref, k_ref, v_ref,
):
    heads = q_ref.shape[1] // PAD
    span = heads * PAD
    width = x_ref.shape[1]
    x = x_ref[...].astype(jnp.float32)
    rms = lax.rsqrt(jnp.mean(x * x, axis=-1, keepdims=True) + EPSILON)
    shift_by = mod_ref[0, :, :width]
    scale_by = mod_ref[0, :, width:]
    normed = (x * rms * (1.0 + scale_by) + shift_by).astype(jnp.bfloat16)
    normed_ref[...] = normed
    cosine, front, back = cos_ref[...], front_ref[...], back_ref[...]
    q_gain, k_gain = gain_ref[0:1, :], gain_ref[1:2, :]
    for part, w_ref in enumerate((wq_ref, wk_ref, wv_ref)):
        lin = full_dot(normed, w_ref[...])
        for h in range(heads):
            cols = slice(h * PAD, (h + 1) * PAD)
            piece = lin[:, cols]
            extra = extra_ref[0, part : part + 1, :]
            if part == 2:
                v_ref[:, cols] = (piece + extra).astype(jnp.bfloat16)
                continue
            lin_ref[:, part * span + h * PAD : part * span + (h + 1) * PAD] = piece.astype(
                jnp.bfloat16
            )
            gain = q_gain if part == 0 else k_gain
            turned = rotate(piece * head_inverse(piece) * gain, cosine, front, back)
            out_ref = q_ref if part == 0 else k_ref
            out_ref[:, cols] = (turned + extra).astype(jnp.bfloat16)


def prepare(x, mods, weights, tables, gains, extras):
    rows, width = x.shape
    span = weights[0].shape[1]
    blocks = rows // SLOT_TOK
    row_block = lambda cols: pl.BlockSpec((SLOT_TOK, cols), lambda i: (i, 0))
    whole = lambda arr: pl.BlockSpec(arr.shape, lambda i: (0,) * arr.ndim)
    out = lambda cols: jax.ShapeDtypeStruct((rows, cols), jnp.bfloat16)
    return pl.pallas_call(
        prepare_kernel,
        grid=(blocks,),
        in_specs=[
            row_block(width),
            pl.BlockSpec((1, 1, 2 * width), lambda i: (i, 0, 0)),
            *(whole(w) for w in weights),
            row_block(PAD), row_block(PAD), row_block(PAD),
            whole(gains),
            pl.BlockSpec((1, 3, PAD), lambda i: (i, 0, 0)),
        ],
        out_specs=[row_block(width), row_block(2 * span), row_block(span), row_block(span), row_block(span)],
        out_shape=[out(width), out(2 * span), out(span), out(span), out(span)],
        compiler_params=pltpu.CompilerParams(vmem_limit_bytes=VMEM_LIMIT),
        cost_estimate=pl.CostEstimate(
            flops=6 * rows * width * span, bytes_accessed=2 * (rows * (2 * width + 5 * span) + 3 * width * span),
            transcendentals=0,
        ),
    )(x, mods, *weights, *tables, gains, extras)


def split_lanes(values, first_lane, shape):
    lane = lax.broadcasted_iota(jnp.int32, shape, 1)
    high = values.astype(jnp.bfloat16).astype(jnp.float32)
    rest = values - high
    mid = rest.astype(jnp.bfloat16).astype(jnp.float32)
    low = rest - mid
    return jnp.where(
        lane == first_lane, high, jnp.where(lane == first_lane + 1, mid, jnp.where(lane == first_lane + 2, low, 0.0))
    )


def attend_kernel(q_ref, kn_ref, kf_ref, vn_ref, vf_ref, mixed_ref, qlog_ref, *, step):
    keys = (kn_ref[...], kf_ref[...])
    values = (vn_ref[...], vf_ref[...])
    for first in range(0, q_ref.shape[0], step):
        rows = slice(first, first + step)
        q = q_ref[rows, :]
        total = None
        for key, value in zip(keys, values):
            weight = jnp.exp2(full_dot(q, key, CONTRACT_COLS) * SCORE_LOG2).astype(jnp.bfloat16)
            term = full_dot(weight, value)
            total = term if total is None else total + term
        row_sum = total[:, TOTAL_LANE : TOTAL_LANE + 1]
        mixed_ref[rows, :] = (total * (1.0 / row_sum)).astype(jnp.bfloat16)
        log_sum = jnp.log2(row_sum) * (-1.0 / SCORE_LOG2)
        qlog_ref[rows, :] = (q.astype(jnp.float32) + split_lanes(log_sum, LOG_LANE, q.shape)).astype(
            jnp.bfloat16
        )


def attend(q, kn, kf, vn, vf, step=256):
    rows, span = q.shape
    heads = span // PAD
    block = lambda arr: pl.BlockSpec((arr.shape[0], PAD), lambda h: (0, h))
    return pl.pallas_call(
        functools.partial(attend_kernel, step=step),
        grid=(heads,),
        in_specs=[block(a) for a in (q, kn, kf, vn, vf)],
        out_specs=[block(q), block(q)],
        out_shape=[jax.ShapeDtypeStruct(q.shape, jnp.bfloat16)] * 2,
        compiler_params=pltpu.CompilerParams(vmem_limit_bytes=VMEM_LIMIT),
        cost_estimate=pl.CostEstimate(
            flops=4 * rows * (kn.shape[0] + kf.shape[0]) * span, bytes_accessed=2 * (3 * rows * span + 4 * kn.shape[0] * span),
            transcendentals=rows * (kn.shape[0] + kf.shape[0]) * heads,
        ),
    )(q, kn, kf, vn, vf)


def unturn(grad, lin, gain, cosine, front, back):
    turned = rotate(grad, cosine, -front, -back)
    inverse = head_inverse(lin)
    normed = lin * inverse
    gained = turned * gain
    mean = jnp.sum(gained * normed, axis=-1, keepdims=True) * (1.0 / HEAD_DIM)
    return inverse * (gained - normed * mean), jnp.sum(turned * normed, axis=0, keepdims=True)


def pull_kernel(*refs, final):
    if final:
        (ga_ref, mixed_ref, q_ref, kn_ref, kf_ref, vn_ref, vf_ref, wo_ref, squeeze_ref, gain_ref,
         cos_ref, front_ref, back_ref, qlin_ref, klin_ref, acck_ref, accv_ref, near_ref, gains_in_ref,
         out_ref, gains_ref, dk_ref, dv_ref, dq_ref) = refs
    else:
        (ga_ref, mixed_ref, q_ref, kn_ref, kf_ref, vn_ref, vf_ref, wo_ref, squeeze_ref, gain_ref,
         cos_ref, front_ref, back_ref, qlin_ref,
         out_ref, gains_ref, dk_ref, dv_ref) = refs
    heads = q_ref.shape[1] // PAD
    half = kn_ref.shape[0]
    step = pl.program_id(0)
    rows = ga_ref.shape[0]

    @pl.when(step == 0)
    def _():
        if final:
            dk_ref[...] = acck_ref[...]
            dv_ref[...] = accv_ref[...]
            gains_ref[...] = gains_in_ref[...]
        else:
            dk_ref[...] = jnp.zeros_like(dk_ref)
            dv_ref[...] = jnp.zeros_like(dv_ref)
            gains_ref[...] = jnp.zeros_like(gains_ref)

    if final:
        first = pl.multiple_of(half + step * rows, rows)
        table_rows = pl.ds(first, rows)
    else:
        table_rows = slice(None)
    cosine, front, back = cos_ref[table_rows, :], front_ref[table_rows, :], back_ref[table_rows, :]
    grad_mixed = full_dot(ga_ref[...], wo_ref[...], CONTRACT_COLS).astype(jnp.bfloat16)
    gain_sum = jnp.zeros((1, PAD), jnp.float32)
    q_grads = []
    for h in range(heads):
        cols = slice(h * PAD, (h + 1) * PAD)
        grad_low = grad_mixed[:, cols]
        grad_head = grad_low.astype(jnp.float32)
        mixed = mixed_ref[:, cols].astype(jnp.float32)
        row_dot = jnp.sum(grad_head * mixed, axis=-1, keepdims=True)
        grad_aug = (grad_head + split_lanes(-row_dot, DOT_LANE, grad_head.shape)).astype(jnp.bfloat16)
        q = q_ref[:, cols]
        dq = None
        for part, (key_ref, value_ref) in enumerate(((kn_ref, vn_ref), (kf_ref, vf_ref))):
            key, value = key_ref[:, cols], value_ref[:, cols]
            key_rows = slice(part * half, (part + 1) * half)
            probs = jnp.exp2(full_dot(key, q, CONTRACT_COLS) * SCORE_LOG2)
            grad_probs = full_dot(value, grad_aug, CONTRACT_COLS)
            grad_scores = (probs * grad_probs).astype(jnp.bfloat16)
            dv_ref[key_rows, cols] += full_dot(probs.astype(jnp.bfloat16), grad_low)
            dk_ref[key_rows, cols] += full_dot(grad_scores, q)
            term = full_dot(grad_scores, key, CONTRACT_ROWS)
            dq = term if dq is None else dq + term
        lin = qlin_ref[:, cols].astype(jnp.float32)
        grad_lin, gain_term = unturn(dq * INV_ROOT, lin, gain_ref[0:1, :], cosine, front, back)
        gain_sum = gain_sum + gain_term
        q_grads.append(grad_lin.astype(jnp.bfloat16))
    gains_ref[0:1, :] += gain_sum
    q_compact = full_dot(jnp.concatenate(q_grads, axis=1), squeeze_ref[...]).astype(jnp.bfloat16)
    if not final:
        out_ref[...] = q_compact
        return
    dq_ref[pl.ds(pl.multiple_of(step * rows, rows), rows), :] = q_compact

    @pl.when(step == pl.num_programs(0) - 1)
    def _():
        key_gain = jnp.zeros((1, PAD), jnp.float32)
        for block in range(2 * half // rows):
            span = slice(block * rows, (block + 1) * rows)
            k_grads = []
            for h in range(heads):
                cols = slice(h * PAD, (h + 1) * PAD)
                grad_lin, gain_term = unturn(
                    dk_ref[span, cols] * INV_ROOT, klin_ref[span, cols].astype(jnp.float32),
                    gain_ref[1:2, :], cos_ref[span, :], front_ref[span, :], back_ref[span, :],
                )
                key_gain += gain_term
                k_grads.append(grad_lin.astype(jnp.bfloat16))
            k_compact = full_dot(jnp.concatenate(k_grads, axis=1), squeeze_ref[...]).astype(jnp.bfloat16)
            v_compact = full_dot(dv_ref[span, :].astype(jnp.bfloat16), squeeze_ref[...]).astype(jnp.bfloat16)
            if block * rows < half:
                q_part = near_ref[span, :]
            else:
                q_part = dq_ref[block * rows - half : block * rows - half + rows, :]
            out_ref[span, :] = jnp.concatenate([q_part, k_compact, v_compact], axis=1)
        gains_ref[1:2, :] += key_gain


def pull(ga, mixed, qlog, kn, kf, vn, vf, w_out, squeeze, gains, tables, q_lin, k_lin=None, carried=None):
    final = carried is not None
    rows, width = ga.shape
    span = qlog.shape[1]
    half = kn.shape[0]
    compact = squeeze.shape[1]
    block = 256
    row_block = lambda cols: pl.BlockSpec((block, cols), lambda i: (i, 0))
    whole = lambda arr: pl.BlockSpec(arr.shape, lambda i: (0,) * arr.ndim)
    fixed = lambda shape: pl.BlockSpec(shape, lambda i: (0,) * len(shape))
    args = [ga, mixed, qlog, kn, kf, vn, vf, w_out, squeeze, gains, *tables, q_lin]
    specs = [row_block(width), row_block(span), row_block(span)] + [whole(a) for a in (kn, kf, vn, vf, w_out, squeeze, gains)]
    acc = jax.ShapeDtypeStruct((2 * half, span), jnp.float32)
    gain_shape = jax.ShapeDtypeStruct((8, PAD), jnp.float32)
    if final:
        specs += [whole(t) for t in tables] + [row_block(span)]
        near_q, gain_in, acc_k, acc_v = carried
        args += [k_lin, acc_k, acc_v, near_q, gain_in]
        specs += [whole(a) for a in (k_lin, acc_k, acc_v, near_q, gain_in)]
        out_shape = [jax.ShapeDtypeStruct((2 * half, 3 * compact), jnp.bfloat16), gain_shape]
        out_specs = [fixed((2 * half, 3 * compact)), fixed((8, PAD))]
        scratch = [pltpu.VMEM(acc.shape, jnp.float32), pltpu.VMEM(acc.shape, jnp.float32), pltpu.VMEM((rows, compact), jnp.bfloat16)]
    else:
        specs += [row_block(PAD) for t in tables] + [row_block(span)]
        out_shape = [jax.ShapeDtypeStruct((rows, compact), jnp.bfloat16), gain_shape, acc, acc]
        out_specs = [row_block(compact), fixed((8, PAD)), fixed(acc.shape), fixed(acc.shape)]
        scratch = []
    return pl.pallas_call(
        functools.partial(pull_kernel, final=final),
        grid=(rows // block,),
        in_specs=specs, out_specs=out_specs, out_shape=out_shape, scratch_shapes=scratch,
        compiler_params=pltpu.CompilerParams(vmem_limit_bytes=VMEM_LIMIT),
        cost_estimate=pl.CostEstimate(
            flops=10 * rows * 2 * half * span, bytes_accessed=2 * rows * (width + 3 * span) + 16 * half * span,
            transcendentals=rows * 2 * half * span // PAD,
        ),
    )(*args)


def swap(values, axis_name, bit):
    count = lax.axis_size(axis_name)
    return lax.ppermute(values, axis_name, [(i, i ^ bit) for i in range(count)])


def after(values, *earlier):
    return lax.optimization_barrier((values, *earlier))[0]


def bits_of(axis_name):
    count = lax.axis_size(axis_name)
    bits = []
    bit = 1
    while bit < count:
        bits.append(bit)
        bit *= 2
    assert bit == count
    return bits


def gather_dp(values):
    for bit in reversed(bits_of("dp")):
        values = jnp.concatenate([values, swap(values, "dp", bit)], axis=0)
    return values


def reduce_dp(grad, bits, splits, anchors):
    place = lax.axis_index("dp")
    anchors = list(anchors)

    def tied(values):
        return after(values, *anchors.pop(0)) if anchors else values

    low = grad
    for bit in bits:
        half = low.shape[0] // 2
        upper = (place // bit) % 2
        mine = lax.dynamic_slice_in_dim(low, upper * half, half, 0)
        other = lax.dynamic_slice_in_dim(low, (1 - upper) * half, half, 0)
        got = swap(other, "dp", bit)
        mine = tied(mine)
        low = (mine.astype(jnp.float32) + got.astype(jnp.float32)).astype(jnp.bfloat16)
    for bit in reversed(bits):
        upper = (place // bit) % 2
        got = swap(low, "dp", bit)
        low = tied(low)
        if bit == bits[0]:
            break
        low = jnp.where(
            upper == 1,
            jnp.concatenate([got, low], axis=0),
            jnp.concatenate([low, got], axis=0),
        )
    outs = []
    first = 0
    for width in splits:
        one, two = got[:, first : first + width], low[:, first : first + width]
        outs.append(
            jnp.where(
                upper == 1, jnp.concatenate([one, two], axis=0), jnp.concatenate([two, one], axis=0)
            ).astype(jnp.float32)
        )
        first += width
    return outs


def rows_dot(source, weight):
    return jnp.dot(source, weight, preferred_element_type=jnp.float32)


def dot_cols(source, weight):
    return lax.dot_general(source, weight, CONTRACT_COLS, preferred_element_type=jnp.float32)


def dot_rows(left, right):
    return lax.dot_general(
        left, right, CONTRACT_ROWS, preferred_element_type=jnp.float32
    ).astype(jnp.bfloat16)


def gather_halves(own):
    far_own = swap(own, "tensor", 2)
    near = jnp.concatenate([own, swap(own, "tensor", 1)], axis=0)
    far = jnp.concatenate([far_own, swap(far_own, "tensor", 1)], axis=0)
    return near, far


def send_far(far):
    low = far.astype(jnp.bfloat16)
    got = swap(low[SLOT_TOK:], "tensor", 1)
    total = low[:SLOT_TOK].astype(jnp.float32) + got.astype(jnp.float32)
    return swap(total.astype(jnp.bfloat16), "tensor", 2)


def sum_near(near, far_got):
    low = near.astype(jnp.bfloat16)
    got = swap(low[SLOT_TOK:], "tensor", 1)
    return low[:SLOT_TOK].astype(jnp.float32) + got.astype(jnp.float32) + far_got.astype(jnp.float32)


def rope_tables(grid_row, grid_col):
    quarter = HEAD_DIM // 4
    lane = jnp.arange(PAD, dtype=jnp.int32)
    rates = jnp.exp(-math.log(10000.0) * (lane % quarter).astype(jnp.float32) / quarter)
    position = jnp.where(lane[None] < 2 * quarter, grid_row[:, None], grid_col[:, None])
    angles = position.astype(jnp.float32) * rates[None]
    valid = (lane < HEAD_DIM)[None]
    is_front = ((lane % (2 * quarter)) < quarter)[None]
    cosine, sine_v = jnp.cos(angles), jnp.sin(angles)
    return (
        jnp.where(valid, cosine, 0.0),
        jnp.where(valid & is_front, -sine_v, 0.0),
        jnp.where(valid & ~is_front, sine_v, 0.0),
    )


def lane_extras(slot_ids, item_count):
    lane = jnp.arange(PAD, dtype=jnp.int32)
    hot = (lane - ITEM_LANE)[None] == (slot_ids + 1)[:, None]
    item_lane = ((lane >= ITEM_LANE) & (lane <= ITEM_LANE + item_count))[None]
    log_lane = ((lane >= LOG_LANE) & (lane < LOG_LANE + 3))[None]
    for_key = jnp.where(item_lane & ~hot, -FAR_ITEM, 0.0) + jnp.where(log_lane, 1.0, 0.0)
    for_value = jnp.broadcast_to(((lane >= TOTAL_LANE) & (lane < DOT_LANE + 3))[None], hot.shape)
    return jnp.stack([hot.astype(jnp.float32), for_key, for_value.astype(jnp.float32)], axis=1)


def local(
    tokens,
    w_query,
    w_key,
    w_value,
    w_out,
    w_gate,
    w_up,
    w_down,
    w_mod,
    b_mod,
    class_table,
    q_gain,
    k_gain,
    slot_item,
    labels,
    tsteps,
    cotangent,
):
    tensor_count = lax.axis_size("tensor")
    tensor_place = lax.axis_index("tensor")
    slot_count = slot_item.shape[1]
    item_count = labels.shape[1]
    assert tensor_count == 4 and slot_count == 4 and item_count < LOG_LANE - ITEM_LANE
    width = tokens.shape[1]
    head_cols = w_query.shape[1]
    heads = head_cols // HEAD_DIM
    bias_len = b_mod.shape[0]
    slot_ids = slot_item[0]
    half = 2 * SLOT_TOK

    tokens_near, tokens_far = gather_halves(tokens)
    cot_near, cot_far = gather_halves(after(cotangent, tokens_far))

    slots = jnp.arange(slot_count, dtype=jnp.int32)
    rel_hot = (tensor_place ^ slots)[:, None] == slots[None, :]
    rel_int = rel_hot.astype(jnp.int32)
    item_ids = jnp.arange(item_count, dtype=jnp.int32)
    class_ids = jnp.arange(class_table.shape[0], dtype=jnp.int32)

    def condition(label_ids, step_ids):
        label_hot = (label_ids[:, None] == class_ids[None, :]).astype(jnp.float32)
        embedded = rows_dot(label_hot.astype(jnp.bfloat16), class_table)
        cond_pre = embedded + sinusoid(step_ids, tensor_place * head_cols, head_cols)
        return label_hot, cond_pre

    _, cond_own = condition(labels[0], tsteps[0])
    bias_full = lax.dynamic_update_slice_in_dim(
        jnp.zeros((6 * width,), jnp.float32), b_mod, tensor_place * bias_len, 0
    )
    modul = rows_dot(jax.nn.silu(cond_own).astype(jnp.bfloat16), w_mod) + bias_full[None, :]
    modul = modul + swap(modul, "tensor", 1)
    modul = modul + swap(modul, "tensor", 2)
    rel_ids = jnp.sum(rel_int * slot_ids[None, :], axis=1)
    rel_pick = (rel_ids[:, None] == item_ids[None, :]).astype(jnp.float32)
    per_slot = jnp.dot(rel_pick, modul, precision=lax.Precision.HIGHEST)
    shift_a, scale_a, gate_a, shift_m, scale_m, gate_m = jnp.split(per_slot[:1], 6, axis=1)
    gate_m_all = per_slot[:, 5 * width :]

    grid_row, grid_col = grid_positions(slot_ids)

    def rel_tokens(per_token):
        return jnp.sum(rel_int[:, :, None] * per_token.reshape(1, slot_count, SLOT_TOK), axis=1).reshape(-1)

    tables = rope_tables(rel_tokens(grid_row), rel_tokens(grid_col))
    extras = lane_extras(rel_ids, item_count)
    gains = jnp.pad(jnp.stack([q_gain, k_gain]), ((0, 0), (0, PAD - HEAD_DIM)))
    pad_row = jnp.arange(heads * PAD, dtype=jnp.int32)[:, None]
    flat_col = jnp.arange(head_cols, dtype=jnp.int32)[None, :]
    squeeze = (
        (pad_row // PAD == flat_col // HEAD_DIM) & (pad_row % PAD == flat_col % HEAD_DIM)
    ).astype(jnp.bfloat16)
    w_wide = [dot_cols(w, squeeze).astype(jnp.bfloat16) for w in (w_query, w_key, w_value)]
    w_out_wide = rows_dot(squeeze, w_out).astype(jnp.bfloat16)
    w_qkv = jnp.concatenate([w_query, w_key, w_value], axis=1)
    w_gate_up = jnp.concatenate([w_gate, w_up], axis=1)

    mods = per_slot[:, None, : 2 * width]
    near_tables = [t[:half] for t in tables]
    far_tables = [t[half:] for t in tables]
    attn_near, lin_near, q_near, k_near, v_near = prepare(
        tokens_near, mods[:2], w_wide, near_tables, gains, extras[:2]
    )
    attn_far, lin_far, q_far, k_far, v_far = prepare(
        tokens_far, mods[2:], w_wide, far_tables, gains, extras[2:]
    )
    mixed_far, qlog_far = attend(q_far, k_near, k_far, v_near, v_far)
    far_got = send_far(rows_dot(mixed_far, w_out_wide))
    mixed_near, qlog_near = attend(q_near, k_near, k_far, v_near, v_far)
    attn = sum_near(rows_dot(mixed_near, w_out_wide), far_got)

    resid = tokens.astype(jnp.float32)
    middle = resid + gate_a * attn

    def norm_rows(values, shift_by, scale_by):
        return modulated_norm(values[None], shift_by, scale_by)[0]

    normed_two, norm_two_back = jax.vjp(norm_rows, middle, shift_m, scale_m)
    mlp_near, mlp_far = gather_halves(normed_two.astype(jnp.bfloat16))

    def swiglu(gate_part, up_part):
        return jax.nn.silu(gate_part) * up_part

    def mlp_rows(rows, cot_rows, gates):
        gate_lin, up_lin = jnp.split(rows_dot(rows, w_gate_up), 2, axis=1)
        hidden_f, swiglu_back = jax.vjp(swiglu, gate_lin, up_lin)
        grad_branch = (
            (gates[:, None, :] * cot_rows.astype(jnp.float32).reshape(2, SLOT_TOK, width))
            .astype(jnp.bfloat16)
            .reshape(half, width)
        )
        grad_gate, grad_up = swiglu_back(dot_cols(grad_branch, w_down))
        grad_gate_up = jnp.concatenate([grad_gate, grad_up], axis=1).astype(jnp.bfloat16)
        return hidden_f.astype(jnp.bfloat16), grad_branch, grad_gate_up

    hidden_near, branch_grad_near, gu_near = mlp_rows(mlp_near, cot_near, gate_m_all[:2])
    hidden_far, branch_grad_far, gu_far = mlp_rows(mlp_far, cot_far, gate_m_all[2:])
    far_got = send_far(dot_cols(gu_far, w_gate_up))
    grad_normed_mlp = sum_near(dot_cols(gu_near, w_gate_up), far_got)

    grad_out = cotangent.astype(jnp.float32)
    grad_mid_norm, grad_shift_m, grad_scale_m = norm_two_back(grad_normed_mlp)
    grad_middle = grad_out + grad_mid_norm
    grad_gate_a = jnp.sum(attn * grad_middle, axis=0, keepdims=True)
    ga_near, ga_far = gather_halves((gate_a * grad_middle).astype(jnp.bfloat16))
    q_grad_near, gain_near, acc_k, acc_v = pull(
        ga_near, mixed_near, qlog_near, k_near, k_far, v_near, v_far, w_out_wide, squeeze, gains,
        near_tables, lin_near[:, : heads * PAD],
    )
    k_lin = jnp.concatenate([lin_near[:, heads * PAD :], lin_far[:, heads * PAD :]], axis=0)
    grad_qkv, gain_grads = pull(
        ga_far, mixed_far, qlog_far, k_near, k_far, v_near, v_far, w_out_wide, squeeze, gains,
        tables, lin_far[:, : heads * PAD], k_lin, (q_grad_near, gain_near, acc_k, acc_v),
    )
    far_got = send_far(dot_cols(grad_qkv[half:], w_qkv))
    grad_normed_attn = sum_near(dot_cols(grad_qkv[:half], w_qkv), far_got)

    both = lambda near, far: jnp.concatenate([near, far], axis=0)
    attn_all = both(attn_near, attn_far)
    mlp_all = both(mlp_near, mlp_far)
    hidden = both(hidden_near, hidden_far)
    branch_grad = both(branch_grad_near, branch_grad_far)
    bits = bits_of("dp")
    late_first = bits[1:] + bits[:1]
    (grad_w_down,) = reduce_dp(
        dot_rows(hidden, branch_grad), late_first, [width],
        [(q_grad_near,), (grad_qkv,), (grad_qkv,), (grad_normed_attn,)],
    )
    grad_w_gate, grad_w_up = reduce_dp(
        dot_rows(mlp_all, both(gu_near, gu_far)), bits, [w_gate.shape[1], w_up.shape[1]],
        [(grad_qkv,), (grad_normed_attn,)],
    )
    grad_w_out_wide = dot_rows(both(mixed_near, mixed_far), both(ga_near, ga_far))
    grad_w_out_low = grad_w_out_wide.reshape(heads, PAD, width)[:, :HEAD_DIM].reshape(head_cols, width)
    (grad_w_out,) = reduce_dp(grad_w_out_low, bits, [width], [(grad_normed_attn,)])
    grad_w_query, grad_w_key, grad_w_value = reduce_dp(
        dot_rows(attn_all, grad_qkv), bits, [head_cols] * 3, [(grad_normed_attn,)]
    )

    far_got = send_far(rows_dot(after(hidden_far, ga_far), w_down))
    branch = sum_near(rows_dot(after(hidden_near, ga_far), w_down), far_got)
    output = (middle + gate_m * branch).astype(jnp.bfloat16)
    grad_gate_m = jnp.sum(branch * grad_out, axis=0, keepdims=True)

    _, norm_one_back = jax.vjp(norm_rows, resid, shift_a, scale_a)
    grad_resid_norm, grad_shift_a, grad_scale_a = norm_one_back(grad_normed_attn)
    grad_tokens = (grad_middle + grad_resid_norm).astype(jnp.bfloat16)

    grad_slot = jnp.concatenate(
        [
            grad_shift_a,
            grad_scale_a,
            grad_gate_a,
            grad_shift_m,
            grad_scale_m,
            grad_gate_m,
            gain_grads[:1],
            gain_grads[1:2],
        ],
        axis=1,
    )
    pair_slots = jnp.concatenate([grad_slot, swap(grad_slot, "tensor", 2)], axis=0)
    grad_slots = jnp.concatenate([pair_slots, swap(pair_slots, "tensor", 1)], axis=0)
    mod_width = 6 * width
    pick_order = jnp.stack([rel_pick[0], rel_pick[2], rel_pick[1], rel_pick[3]])
    grad_items = lax.dot_general(
        pick_order,
        grad_slots[:, :mod_width],
        CONTRACT_ROWS,
        precision=lax.Precision.HIGHEST,
        preferred_element_type=jnp.float32,
    ).astype(jnp.bfloat16)
    gain_sum = jnp.sum(grad_slots[:, mod_width:], axis=0, keepdims=True)
    gain_rows = jnp.pad(gain_sum, ((0, item_count - 1), (0, 0))).astype(jnp.bfloat16)
    items_all = gather_dp(jnp.concatenate([grad_items, gain_rows], axis=1))
    ids_all = gather_dp(
        jnp.stack([after(labels[0], gate_m), after(tsteps[0], gate_m)], axis=1)
    )
    grad_modul_low = items_all[:, :mod_width]
    gain_total = jnp.sum(items_all[:, mod_width:].astype(jnp.float32), axis=0)
    grad_q_gain = gain_total[:HEAD_DIM]
    grad_k_gain = gain_total[PAD : PAD + HEAD_DIM]
    label_hot, cond_pre = condition(ids_all[:, 0], ids_all[:, 1])
    cond_full, silu_back = jax.vjp(jax.nn.silu, cond_pre)
    grad_w_mod = lax.dot_general(
        cond_full.astype(jnp.bfloat16), grad_modul_low, CONTRACT_ROWS, preferred_element_type=jnp.float32
    )
    grad_bias_full = jnp.sum(grad_modul_low.astype(jnp.float32), axis=0)
    grad_b_mod = lax.dynamic_slice_in_dim(grad_bias_full, tensor_place * bias_len, bias_len, 0)
    grad_cond_pre = silu_back(dot_cols(grad_modul_low, w_mod))[0]
    grad_class_table = lax.dot_general(
        label_hot,
        grad_cond_pre,
        CONTRACT_ROWS,
        precision=lax.Precision.HIGHEST,
        preferred_element_type=jnp.float32,
    )
    return (
        output,
        grad_tokens,
        grad_w_query,
        grad_w_key,
        grad_w_value,
        grad_w_out,
        grad_w_gate,
        grad_w_up,
        grad_w_down,
        grad_w_mod,
        grad_b_mod,
        grad_class_table,
        grad_q_gain,
        grad_k_gain,
    )


def solution(mesh):
    in_specs = (
        P(("dp", "tensor"), None),
        P(None, "tensor"),
        P(None, "tensor"),
        P(None, "tensor"),
        P("tensor", None),
        P(None, "tensor"),
        P(None, "tensor"),
        P("tensor", None),
        P("tensor", None),
        P("tensor"),
        P(None, "tensor"),
        P(),
        P(),
        P("dp", None),
        P("dp", None),
        P("dp", None),
        P(("dp", "tensor"), None),
    )
    out_specs = (
        P(("dp", "tensor"), None),
        P(("dp", "tensor"), None),
        P(None, "tensor"),
        P(None, "tensor"),
        P(None, "tensor"),
        P("tensor", None),
        P(None, "tensor"),
        P(None, "tensor"),
        P("tensor", None),
        P("tensor", None),
        P("tensor"),
        P(None, "tensor"),
        P(),
        P(),
    )
    return jax.shard_map(local, mesh=mesh, in_specs=in_specs, out_specs=out_specs, check_vma=False)
```

time: 512 us -> 520 us (1.016)
  Pallas kernels: 0 us -> 60.7 us
  waiting for transfers between devices: 231 us -> 192 us
  matrix products: 93.3 us -> 55.8 us
  local copies, waits for them, and re-layouts: 44.1 us -> 72.2 us
    pallas_call x0 -> x6, Pallas kernels: none -> 60.7 us  [the longest x2 34.6 us: pull(): pl.pallas_call(functools.partial(pull_kernel, final=final), grid=(rows //...]
    ppermute x59 -> x58, waiting for transfers between devices: 231 us -> 192 us  [swap(): return lax.ppermute(values, axis_name, [(i, i ^ bit) for i in range(count)])]
    dot_general x10 -> x2, matrix products: 41.4 us -> 4.9 us  [the longest x1 4.49 us: local(): lax.dot_general(cond_full.astype(jnp.bfloat16), grad_modul_low, CONTRACT_...]
    unnamed x258 -> x191, local copies, waits for them, and re-layouts: 13.2 us -> 25.9 us
    slice x10 -> x25, local copies, waits for them, and re-layouts: 4.76 us -> 17.4 us  [the longest x4 5.57 us: reduce_dp(): one, two = (got[:, first:first + width], low[:, first:first + width])]
    dynamic_slice x0 -> x7, local copies, waits for them, and re-layouts: none -> 10.6 us  [reduce_dp(): mine = lax.dynamic_slice_in_dim(low, upper * half, half, 0)]
    reduce_sum x6 -> x2, other arithmetic: 10.4 us -> 1.43 us  [the longest x1 1.4 us: local(): grad_gate_a = jnp.sum(attn * grad_middle, axis=0, keepdims=True)]
    select_n x8, other arithmetic: 8.51 us -> 14.7 us  [reduce_dp(): jnp.where(upper == 1, jnp.concatenate([got, low], axis=0), jnp.concatenat...]
  transfers between devices with their start and end apart: 59 -> 58, of which waited for: 26 -> 18; matrix products, arithmetic and copies ran while one was open for 30% -> 35% of each run, Pallas kernels for 0% -> 12%
where the time goes in v2:
time: 520 us; the launch traced here: 510 us
  waiting for transfers between devices  192 us (37%)
  other arithmetic  77.4 us (15%)
  local copies, waits for them, and re-layouts  72.2 us (14%)
  Pallas kernels  60.7 us (12%)
  matrix products  55.8 us (11%)
  starting transfers between devices  50 us (10%)
    ppermute x58, waiting for transfers between devices, swap(): return lax.ppermute(values, axis_name, [(i, i ^ bit) for i in range(count)])  192 us
    ppermute x58, starting transfers between devices, swap(): return lax.ppermute(values, axis_name, [(i, i ^ bit) for i in range(count)])  50 us
    pallas_call x2, Pallas kernels, pull(): pl.pallas_call(functools.partial(pull_kernel, final=final), grid=(rows //...  34.6 us
    unnamed x191, local copies, waits for them, and re-layouts  25.9 us
    dot_general x10, matrix products, dot_cols(): lax.dot_general(source, weight, CONTRACT_COLS, preferred_element_type=jnp...  20.9 us
    convert_element_type x7, other arithmetic, reduce_dp(): outs.append(jnp.where(upper == 1, jnp.concatenate([one, two], axis=0), jn...  16.7 us
    dot_general x9, matrix products, rows_dot(): return jnp.dot(source, weight, preferred_element_type=jnp.float32)  16.6 us
    select_n x8, other arithmetic, reduce_dp(): jnp.where(upper == 1, jnp.concatenate([got, low], axis=0), jnp.concatenat...  14.7 us
  transfers between devices with their start and end apart: 58, of which 18 were waited for; matrix products, arithmetic and copies ran while one was open for 35% of the time, Pallas kernels for 12%

profile of v2, /device:TPU:0, one launch (start us, length us, event | category | flops | bytes accessed | tf_op | source)
XLA Modules:
  0.0 509.9 jit_solution(4926623717078409299)
XLA Ops:
  0.7 3.0 collective-permute-start.3
  5.3 4.2 convolution_add_fusion
  32.8 3.6 collective-permute-done.1
  38.0 2.7 collective-permute-start.50
  46.4 6.6 %shard_map.272 = (bf16[512,1152]{1,0:T(8,128)(2,1)}, bf16[512,1024]{1,0:T(8,128)(2,1)}, bf16[512,512]{1,0:T(8,128)(2,1)}, bf16[512,512]{1,0:T(8,128)(2,1)}, bf16[512,512]{1,0:T(8,128)(2,1)}) custom-call(bf16[512,1152]{1,0:T(8,128)(2,1)} %pad_maximum_fusion.x_ref, f32[2,1,2304]{2,1,0:T(1,128)} %slice.196.mod_ref, bf16[1152,512]{1,0:T(8,128)(2,1)} %fusion.7.wq_ref, ...), custom_call_target="tpu_custom_call" | custom-call | flops 1811939328 | bytes 8519680 | tf_op jit(solution)/shard_map/pallas_call | solution.py:113
  55.2 6.6 %shard_map.273 = (bf16[512,1152]{1,0:T(8,128)(2,1)}, bf16[512,1024]{1,0:T(8,128)(2,1)}, bf16[512,512]{1,0:T(8,128)(2,1)}, bf16[512,512]{1,0:T(8,128)(2,1)}, bf16[512,512]{1,0:T(8,128)(2,1)}) custom-call(bf16[512,1152]{1,0:T(8,128)(2,1)} %copy-done.54, f32[2,1,2304]{2,1,0:T(1,128)} %slice.202.mod_ref, bf16[1152,512]{1,0:T(8,128)(2,1)} %fusion.7.wq_ref, ...), custom_call_target="tpu_custom_call" | custom-call | flops 1811939328 | bytes 8519680 | tf_op jit(solution)/shard_map/pallas_call | solution.py:113
  61.9 6.6 %shard_map.275 = (bf16[512,512]{1,0:T(8,128)(2,1)}, bf16[512,512]{1,0:T(8,128)(2,1)}) custom-call(bf16[512,512]{1,0:T(8,128)(2,1)} %get-tuple-element.53.q_ref, bf16[512,512]{1,0:T(8,128)(2,1)} %get-tuple-element.48.kn_ref.refs_3_, bf16[512,512]{1,0:T(8,128)(2,1)} %get-tuple-element.49.kf_ref.refs_4_, bf16[512,512]{1,0:T(8,128)(2,1)} %get-tuple-element.50.vn_ref.refs_5_, ...), custom_call_target="tpu_custom_call" | custom-call | flops 1073741824 | bytes 3670016 | tf_op jit(solution)/shard_map/pallas_call | solution.py:168
  72.6 6.2 %shard_map.274 = (bf16[512,512]{1,0:T(8,128)(2,1)}, bf16[512,512]{1,0:T(8,128)(2,1)}) custom-call(bf16[512,512]{1,0:T(8,128)(2,1)} %get-tuple-element.47.q_ref, bf16[512,512]{1,0:T(8,128)(2,1)} %get-tuple-element.48.kn_ref.refs_3_, bf16[512,512]{1,0:T(8,128)(2,1)} %get-tuple-element.49.kf_ref.refs_4_, bf16[512,512]{1,0:T(8,128)(2,1)} %get-tuple-element.50.vn_ref.refs_5_, ...), custom_call_target="tpu_custom_call" | custom-call | flops 1073741824 | bytes 3670016 | tf_op jit(solution)/shard_map/pallas_call | solution.py:168
  85.1 12.2 %collective-permute-done.7 = bf16[256,1152]{1,0:T(8,128)(2,1)S(1)} collective-permute-done((bf16[256,1152]{1,0:T(8,128)(2,1)S(1)}, bf16[256,1152]{1,0:T(8,128)(2,1)S(1)}, u32[]{:S(2)}, u32[]{:S(2)}) %collective-permute-start.7) | collective-permute-done | bytes 589856 | tf_op jit(solution)/shard_map/ppermute | solution.py:320
  99.9 10.0 %collective-permute-done.11 = bf16[256,1152]{1,0:T(8,128)(2,1)S(1)} collective-permute-done((bf16[256,1152]{1,0:T(8,128)(2,1)S(1)}, bf16[256,1152]{1,0:T(8,128)(2,1)S(1)}, u32[]{:S(2)}, u32[]{:S(2)}) %collective-permute-start.11) | collective-permute-done | bytes 589856 | tf_op jit(solution)/shard_map/ppermute | solution.py:320
  112.5 9.6 %collective-permute-done.13 = bf16[256,1152]{1,0:T(8,128)(2,1)S(1)} collective-permute-done((bf16[256,1152]{1,0:T(8,128)(2,1)S(1)}, bf16[256,1152]{1,0:T(8,128)(2,1)S(1)}, u32[]{:S(2)}, u32[]{:S(2)}) %collective-permute-start.13) | collective-permute-done | bytes 589856 | tf_op jit(solution)/shard_map/ppermute | solution.py:320
  136.9 2.4 convolution_convert_fusion.3
  140.0 12.1 %collective-permute-done.16 = bf16[256,1152]{1,0:T(8,128)(2,1)S(1)} collective-permute-done((bf16[256,1152]{1,0:T(8,128)(2,1)S(1)}, bf16[256,1152]{1,0:T(8,128)(2,1)S(1)}, u32[]{:S(2)}, u32[]{:S(2)}) %collective-permute-start.16) | collective-permute-done | bytes 589856 | tf_op jit(solution)/shard_map/ppermute | solution.py:320
  155.6 3.9 convolution_convert_fusion.1
  164.0 13.0 %shard_map.276 = (bf16[512,288]{1,0:T(8,128)(2,1)}, f32[8,128]{1,0:T(8,128)}, f32[1024,512]{1,0:T(8,128)}, f32[1024,512]{1,0:T(8,128)}) custom-call(bf16[512,1152]{1,0:T(8,128)(2,1)} %pad_maximum_fusion.1.refs_0_, bf16[512,512]{1,0:T(8,128)(2,1)} %get-tuple-element.52.refs_1_, bf16[512,512]{1,0:T(8,128)(2,1)} %get-tuple-element.61.refs_2_, ...), custom_call_target="tpu_custom_call" | custom-call | flops 2684354560 | bytes 6946816 | tf_op jit(solution)/shard_map/pallas_call | solution.py:306
  179.3 2.6 collective-permute-start.45
  184.9 21.6 %shard_map.277 = (bf16[1024,864]{1,0:T(8,128)(2,1)}, f32[8,128]{1,0:T(8,128)}) custom-call(bf16[512,1152]{1,0:T(8,128)(2,1)} %copy-done.17, bf16[512,512]{1,0:T(8,128)(2,1)} %get-tuple-element.54.refs_1_, bf16[512,512]{1,0:T(8,128)(2,1)} %get-tuple-element.58.refs_2_, bf16[512,512]{1,0:T(8,128)(2,1)} %get-tuple-element.48.kn_ref.refs_3_, ...), custom_call_target="tpu_custom_call" | custom-call | flops 2684354560 | bytes 6946816 | tf_op jit(solution)/shard_map/pallas_call | solution.py:306
  206.5 3.5 convolution_convert_fusion.10
  220.8 2.5 convolution_convert_fusion.2
  223.3 2.5 constant_dynamic-slice_fusion.18
  227.4 3.1 add_convert_fusion
  230.5 2.6 convolution_convert_fusion.8
  238.4 2.9 constant_dynamic-slice_fusion.8
  249.7 16.4 %collective-permute-done.26 = bf16[576,864]{1,0:T(8,128)(2,1)S(1)} collective-permute-done((bf16[576,864]{1,0:T(8,128)(2,1)S(1)}, bf16[576,864]{1,0:T(8,128)(2,1)S(1)}, u32[]{:S(2)}, u32[]{:S(2)}) %collective-permute-start.26) | collective-permute-done | bytes 995360 | tf_op jit(solution)/shard_map/ppermute | solution.py:320
  267.7 2.5 copy.52
  273.1 3.7 fusion.58
  279.8 5.9 %collective-permute-done.21 = bf16[256,1152]{1,0:T(8,128)(2,1)S(1)} collective-permute-done((bf16[256,1152]{1,0:T(8,128)(2,1)}, bf16[256,1152]{1,0:T(8,128)(2,1)S(1)}, u32[]{:S(2)}, u32[]{:S(2)}) %collective-permute-start.21) | collective-permute-done | bytes 589856 | tf_op jit(solution)/shard_map/ppermute | solution.py:320
  296.1 2.6 collective-permute-start.40
  308.8 2.4 fusion.54
  313.6 4.1 collective-permute-done.33
  318.8 3.6 collective-permute-start.34
  322.3 14.7 %collective-permute-done.55 = bf16[4,7168]{1,0:T(4,128)(2,1)S(1)} collective-permute-done((bf16[4,7168]{1,0:T(4,128)(2,1)S(1)}, bf16[4,7168]{1,0:T(4,128)(2,1)S(1)}, u32[]{:S(2)}, u32[]{:S(2)}) %collective-permute-start.55) | collective-permute-done | bytes 57376 | tf_op jit(solution)/shard_map/ppermute | solution.py:320
  339.0 3.0 collective-permute-done.56
  343.0 2.7 collective-permute-done.35
  346.5 2.7 maximum_select_fusion.6
  355.9 4.5 fusion.80
  362.5 3.0 collective-permute-start.28
  367.2 26.7 %collective-permute-done.28 = bf16[144,864]{0,1:T(8,128)(2,1)S(1)} collective-permute-done((bf16[144,864]{0,1:T(8,128)(2,1)S(1)}, bf16[144,864]{0,1:T(8,128)(2,1)S(1)}, u32[]{:S(2)}, u32[]{:S(2)}) %collective-permute-start.28) | collective-permute-done | bytes 248864 | tf_op jit(solution)/shard_map/ppermute | solution.py:320
  394.2 2.6 maximum_select_fusion.5
  396.8 2.8 collective-permute-start.42
  401.7 12.9 %collective-permute-done.29 = bf16[144,864]{0,1:T(8,128)(2,1)S(1)} collective-permute-done((bf16[144,864]{0,1:T(8,128)(2,1)S(1)}, bf16[144,864]{0,1:T(8,128)(2,1)S(1)}, u32[]{:S(2)}, u32[]{:S(2)}) %collective-permute-start.29) | collective-permute-done | bytes 248864 | tf_op jit(solution)/shard_map/ppermute | solution.py:320
  419.0 19.1 %collective-permute-done.30 = bf16[288,864]{1,0:T(8,128)(2,1)S(1)} collective-permute-done((bf16[288,864]{1,0:T(8,128)(2,1)}, bf16[288,864]{1,0:T(8,128)(2,1)S(1)}, u32[]{:S(2)}, u32[]{:S(2)}) %collective-permute-start.30) | collective-permute-done | bytes 497696 | tf_op jit(solution)/shard_map/ppermute | solution.py:320
  439.1 2.4 maximum_select_fusion.4
  444.1 3.6 maximum_select_fusion
  448.9 4.2 fusion.34
  455.7 13.5 %collective-permute-done.31 = bf16[576,864]{1,0:T(8,128)(2,1)S(1)} collective-permute-done((bf16[576,864]{1,0:T(8,128)(2,1)}, bf16[576,864]{1,0:T(8,128)(2,1)S(1)}, u32[]{:S(2)}, u32[]{:S(2)}) %collective-permute-start.31) | collective-permute-done | bytes 995360 | tf_op jit(solution)/shard_map/ppermute | solution.py:320
  476.5 2.8 fusion.74
  482.2 21.3 %collective-permute-done.43 = bf16[576,1536]{1,0:T(8,128)(2,1)} collective-permute-done((bf16[576,1536]{1,0:T(8,128)(2,1)}, bf16[576,1536]{1,0:T(8,128)(2,1)}, u32[]{:S(2)}, u32[]{:S(2)}) %collective-permute-start.43) | collective-permute-done | bytes 1769504 | tf_op jit(solution)/shard_map/ppermute | solution.py:320
  (437 shorter events, 179.9 us)
Async XLA Ops:
  0.7 43.5 %collective-permute-start.3 = (bf16[256,1152]{1,0:T(8,128)(2,1)}, bf16[256,1152]{1,0:T(8,128)(2,1)}, u32[]{:S(2)}, u32[]{:S(2)}) collective-permute-start(bf16[256,1152]{1,0:T(8,128)(2,1)} %param.17), channel_id=1, source_target_pairs={{0,2},{1,3},{2,0},{3,1},{4,6},{5,7},{6,4},{7,5},{8,10},{9,11},{10,... | collective-permute-start | bytes 1769480 | tf_op jit(solution)/shard_map/ppermute | solution.py:320
  3.7 40.5 %collective-permute-start.2 = (bf16[256,1152]{1,0:T(8,128)(2,1)}, bf16[256,1152]{1,0:T(8,128)(2,1)}, u32[]{:S(2)}, u32[]{:S(2)}) collective-permute-start(bf16[256,1152]{1,0:T(8,128)(2,1)} %param.17), channel_id=1, source_target_pairs={{0,1},{1,0},{2,3},{3,2},{4,5},{5,4},{6,7},{7,6},{8,9},{9,8},{10,11... | collective-permute-start | bytes 1769480 | tf_op jit(solution)/shard_map/ppermute | solution.py:320
  9.5 21.0 %collective-permute-start = (f32[4,6912]{1,0:T(4,128)}, f32[4,6912]{1,0:T(4,128)}, u32[]{:S(2)}, u32[]{:S(2)}) collective-permute-start(f32[4,6912]{1,0:T(4,128)} %convolution_add_fusion), channel_id=1, source_target_pairs={{0,1},{1,0},{2,3},{3,2},{4,5},{5,4},{6,7},{7,6},{8,9},{9,8},{10,11... | collective-permute-start | bytes 331784 | tf_op jit(solution)/shard_map/ppermute | solution.py:320
  42.6 28.4 %collective-permute-start.51 = (s32[8,2]{0,1:T(2,128)S(1)}, s32[8,2]{0,1:T(2,128)S(1)}, u32[]{:S(2)}, u32[]{:S(2)}) collective-permute-start(s32[8,2]{0,1:T(2,128)S(1)} %pad_add_fusion.1), channel_id=1, source_target_pairs={{0,8},{4,12},{8,0},{12,4},{16,24},{20,28},{24,16},{28,20},{1,9},{5... | collective-permute-start | bytes 200 | tf_op jit(solution)/shard_map/ppermute | solution.py:320
  44.2 9.9 %collective-permute-start.4 = (bf16[256,1152]{1,0:T(8,128)(2,1)}, bf16[256,1152]{1,0:T(8,128)(2,1)S(1)}, u32[]{:S(2)}, u32[]{:S(2)}) collective-permute-start(bf16[256,1152]{1,0:T(8,128)(2,1)} %collective-permute-done.3), channel_id=1, source_target_pairs={{0,1},{1,0},{2,3},{3,2},{4,5},{5,4},{6,7},{7,6},{8,9},{9,8},{10,11... | collective-permute-start | bytes 1769480 | tf_op jit(solution)/shard_map/ppermute | solution.py:320
  70.4 10.5 %collective-permute-start.6 = (bf16[256,1152]{1,0:T(8,128)(2,1)S(1)}, bf16[256,1152]{1,0:T(8,128)(2,1)S(1)}, u32[]{:S(2)}, u32[]{:S(2)}) collective-permute-start(bf16[256,1152]{1,0:T(8,128)(2,1)S(1)} %slice.269), channel_id=1, source_target_pairs={{0,1},{1,0},{2,3},{3,2},{4,5},{5,4},{6,7},{7,6},{8,9},{9,8},{10,11... | collective-permute-start | bytes 1769480 | tf_op jit(solution)/shard_map/ppermute | solution.py:320
  71.1 11.2 %collective-permute-start.52 = (s32[16,2]{0,1:T(2,128)S(1)}, s32[16,2]{0,1:T(2,128)S(1)}, u32[]{:S(2)}, u32[]{:S(2)}) collective-permute-start(s32[16,2]{0,1:T(2,128)S(1)} %pad_add_fusion.2), channel_id=1, source_target_pairs={{0,4},{4,0},{8,12},{12,8},{16,20},{20,16},{24,28},{28,24},{1,5},{5... | collective-permute-start | bytes 392 | tf_op jit(solution)/shard_map/ppermute | solution.py:320
  81.1 16.2 %collective-permute-start.7 = (bf16[256,1152]{1,0:T(8,128)(2,1)S(1)}, bf16[256,1152]{1,0:T(8,128)(2,1)S(1)}, u32[]{:S(2)}, u32[]{:S(2)}) collective-permute-start(bf16[256,1152]{1,0:T(8,128)(2,1)S(1)} %add_convert_fusion.10), channel_id=1, source_target_pairs={{0,2},{1,3},{2,0},{3,1},{4,6},{5,7},{6,4},{7,5},{8,10},{9,11},{10,... | collective-permute-start | bytes 1769480 | tf_op jit(solution)/shard_map/ppermute | solution.py:320
  83.4 29.0 %collective-permute-start.9 = (bf16[256,1152]{1,0:T(8,128)(2,1)S(1)}, bf16[256,1152]{1,0:T(8,128)(2,1)S(1)}, u32[]{:S(2)}, u32[]{:S(2)}) collective-permute-start(bf16[256,1152]{1,0:T(8,128)(2,1)S(1)} %copy-done.7), channel_id=1, source_target_pairs={{0,1},{1,0},{2,3},{3,2},{4,5},{5,4},{6,7},{7,6},{8,9},{9,8},{10,11... | collective-permute-start | bytes 1769480 | tf_op jit(solution)/shard_map/ppermute | solution.py:320
  83.6 26.3 %collective-permute-start.11 = (bf16[256,1152]{1,0:T(8,128)(2,1)S(1)}, bf16[256,1152]{1,0:T(8,128)(2,1)S(1)}, u32[]{:S(2)}, u32[]{:S(2)}) collective-permute-start(bf16[256,1152]{1,0:T(8,128)(2,1)S(1)} %copy-done.7), channel_id=1, source_target_pairs={{0,2},{1,3},{2,0},{3,1},{4,6},{5,7},{6,4},{7,5},{8,10},{9,11},{10,... | collective-permute-start | bytes 1769480 | tf_op jit(solution)/shard_map/ppermute | solution.py:320
  98.1 24.1 %collective-permute-start.13 = (bf16[256,1152]{1,0:T(8,128)(2,1)S(1)}, bf16[256,1152]{1,0:T(8,128)(2,1)S(1)}, u32[]{:S(2)}, u32[]{:S(2)}) collective-permute-start(bf16[256,1152]{1,0:T(8,128)(2,1)S(1)} %add_convert_fusion.9), channel_id=1, source_target_pairs={{0,2},{1,3},{2,0},{3,1},{4,6},{5,7},{6,4},{7,5},{8,10},{9,11},{10,... | collective-permute-start | bytes 1769480 | tf_op jit(solution)/shard_map/ppermute | solution.py:320
  109.9 12.8 %collective-permute-start.12 = (bf16[256,1152]{1,0:T(8,128)(2,1)S(1)}, bf16[256,1152]{1,0:T(8,128)(2,1)S(1)}, u32[]{:S(2)}, u32[]{:S(2)}) collective-permute-start(bf16[256,1152]{1,0:T(8,128)(2,1)S(1)} %collective-permute-done.11), channel_id=1, source_target_pairs={{0,1},{1,0},{2,3},{3,2},{4,5},{5,4},{6,7},{7,6},{8,9},{9,8},{10,11... | collective-permute-start | bytes 1769480 | tf_op jit(solution)/shard_map/ppermute | solution.py:320
  109.9 13.0 %collective-permute-start.8 = (bf16[256,1152]{1,0:T(8,128)(2,1)S(1)}, bf16[256,1152]{1,0:T(8,128)(2,1)S(1)}, u32[]{:S(2)}, u32[]{:S(2)}) collective-permute-start(bf16[256,1152]{1,0:T(8,128)(2,1)S(1)} %add_convert_fusion.9), channel_id=1, source_target_pairs={{0,1},{1,0},{2,3},{3,2},{4,5},{5,4},{6,7},{7,6},{8,9},{9,8},{10,11... | collective-permute-start | bytes 1769480 | tf_op jit(solution)/shard_map/ppermute | solution.py:320
  136.3 15.8 %collective-permute-start.16 = (bf16[256,1152]{1,0:T(8,128)(2,1)S(1)}, bf16[256,1152]{1,0:T(8,128)(2,1)S(1)}, u32[]{:S(2)}, u32[]{:S(2)}) collective-permute-start(bf16[256,1152]{1,0:T(8,128)(2,1)S(1)} %add_convert_fusion.8), channel_id=1, source_target_pairs={{0,2},{1,3},{2,0},{3,1},{4,6},{5,7},{6,4},{7,5},{8,10},{9,11},{10,... | collective-permute-start | bytes 1769480 | tf_op jit(solution)/shard_map/ppermute | solution.py:320
  139.5 37.5 %collective-permute-start.44 = (bf16[384,1152]{1,0:T(8,128)(2,1)S(1)}, bf16[384,1152]{1,0:T(8,128)(2,1)}, u32[]{:S(2)}, u32[]{:S(2)}) collective-permute-start(bf16[384,1152]{1,0:T(8,128)(2,1)S(1)} %get-tuple-element.114), channel_id=1, source_target_pairs={{0,8},{4,12},{8,0},{12,4},{16,24},{20,28},{24,16},{28,20},{1,9},{5... | collective-permute-start | bytes 2654216 | tf_op jit(solution)/shard_map/ppermute | solution.py:320
  159.5 17.5 %collective-permute-start.17 = (bf16[256,1152]{1,0:T(8,128)(2,1)S(1)}, bf16[256,1152]{1,0:T(8,128)(2,1)}, u32[]{:S(2)}, u32[]{:S(2)}) collective-permute-start(bf16[256,1152]{1,0:T(8,128)(2,1)S(1)} %multiply_convert_fusion.4), channel_id=1, source_target_pairs={{0,2},{1,3},{2,0},{3,1},{4,6},{5,7},{6,4},{7,5},{8,10},{9,11},{10,... | collective-permute-start | bytes 1769480 | tf_op jit(solution)/shard_map/ppermute | solution.py:320
  161.5 64.3 %collective-permute-start.38 = (bf16[576,1536]{1,0:T(8,128)(2,1)}, bf16[576,1536]{1,0:T(8,128)(2,1)}, u32[]{:S(2)}, u32[]{:S(2)}) collective-permute-start(bf16[576,1536]{1,0:T(8,128)(2,1)} %get-tuple-element.106), channel_id=1, source_target_pairs={{0,4},{4,0},{8,12},{12,8},{16,20},{20,16},{24,28},{28,24},{1,5},{5... | collective-permute-start | bytes 5308424 | tf_op jit(solution)/shard_map/ppermute | solution.py:320
  179.3 39.0 %collective-permute-start.45 = (bf16[192,1152]{1,0:T(8,128)(2,1)}, bf16[192,1152]{1,0:T(8,128)(2,1)}, u32[]{:S(2)}, u32[]{:S(2)}) collective-permute-start(bf16[192,1152]{1,0:T(8,128)(2,1)} %get-tuple-element.132), channel_id=1, source_target_pairs={{0,16},{4,20},{8,24},{12,28},{16,0},{20,4},{24,8},{28,12},{1,17},{... | collective-permute-start | bytes 1327112 | tf_op jit(solution)/shard_map/ppermute | solution.py:320
  212.4 57.8 %collective-permute-start.23 = (bf16[256,1152]{1,0:T(8,128)(2,1)}, bf16[256,1152]{1,0:T(8,128)(2,1)}, u32[]{:S(2)}, u32[]{:S(2)}) collective-permute-start(bf16[256,1152]{1,0:T(8,128)(2,1)} %slice.281), channel_id=1, source_target_pairs={{0,1},{1,0},{2,3},{3,2},{4,5},{5,4},{6,7},{7,6},{8,9},{9,8},{10,11... | collective-permute-start | bytes 1769480 | tf_op jit(solution)/shard_map/ppermute | solution.py:320
  213.4 27.9 %collective-permute-start.24 = (bf16[256,1152]{1,0:T(8,128)(2,1)}, bf16[256,1152]{1,0:T(8,128)(2,1)}, u32[]{:S(2)}, u32[]{:S(2)}) collective-permute-start(bf16[256,1152]{1,0:T(8,128)(2,1)} %slice.283), channel_id=1, source_target_pairs={{0,1},{1,0},{2,3},{3,2},{4,5},{5,4},{6,7},{7,6},{8,9},{9,8},{10,11... | collective-permute-start | bytes 1769480 | tf_op jit(solution)/shard_map/ppermute | solution.py:320
  215.9 63.9 %collective-permute-start.19 = (bf16[256,1152]{1,0:T(8,128)(2,1)}, bf16[256,1152]{1,0:T(8,128)(2,1)}, u32[]{:S(2)}, u32[]{:S(2)}) collective-permute-start(bf16[256,1152]{1,0:T(8,128)(2,1)} %slice.277), channel_id=1, source_target_pairs={{0,1},{1,0},{2,3},{3,2},{4,5},{5,4},{6,7},{7,6},{8,9},{9,8},{10,11... | collective-permute-start | bytes 1769480 | tf_op jit(solution)/shard_map/ppermute | solution.py:320
  218.5 28.7 %collective-permute-start.20 = (bf16[256,1152]{1,0:T(8,128)(2,1)}, bf16[256,1152]{1,0:T(8,128)(2,1)}, u32[]{:S(2)}, u32[]{:S(2)}) collective-permute-start(bf16[256,1152]{1,0:T(8,128)(2,1)} %slice.279), channel_id=1, source_target_pairs={{0,1},{1,0},{2,3},{3,2},{4,5},{5,4},{6,7},{7,6},{8,9},{9,8},{10,11... | collective-permute-start | bytes 1769480 | tf_op jit(solution)/shard_map/ppermute | solution.py:320
  225.8 18.3 %collective-permute-start.46 = (bf16[96,1152]{1,0:T(8,128)(2,1)}, bf16[96,1152]{1,0:T(8,128)(2,1)}, u32[]{:S(2)}, u32[]{:S(2)}) collective-permute-start(bf16[96,1152]{1,0:T(8,128)(2,1)} %get-tuple-element.143), channel_id=1, source_target_pairs={{0,4},{4,0},{8,12},{12,8},{16,20},{20,16},{24,28},{28,24},{1,5},{5... | collective-permute-start | bytes 663560 | tf_op jit(solution)/shard_map/ppermute | solution.py:320
  241.4 24.7 %collective-permute-start.26 = (bf16[576,864]{1,0:T(8,128)(2,1)S(1)}, bf16[576,864]{1,0:T(8,128)(2,1)S(1)}, u32[]{:S(2)}, u32[]{:S(2)}) collective-permute-start(bf16[576,864]{1,0:T(8,128)(2,1)S(1)} %copy-done.38), channel_id=1, source_target_pairs={{0,4},{4,0},{8,12},{12,8},{16,20},{20,16},{24,28},{28,24},{1,5},{5... | collective-permute-start | bytes 2985992 | tf_op jit(solution)/shard_map/ppermute | solution.py:320
  244.0 27.6 %collective-permute-start.25 = (bf16[256,1152]{1,0:T(8,128)(2,1)}, bf16[256,1152]{1,0:T(8,128)(2,1)}, u32[]{:S(2)}, u32[]{:S(2)}) collective-permute-start(bf16[256,1152]{1,0:T(8,128)(2,1)} %add_convert_fusion.5), channel_id=1, source_target_pairs={{0,2},{1,3},{2,0},{3,1},{4,6},{5,7},{6,4},{7,5},{8,10},{9,11},{10,... | collective-permute-start | bytes 1769480 | tf_op jit(solution)/shard_map/ppermute | solution.py:320
  247.2 46.6 %collective-permute-start.39 = (bf16[288,1536]{1,0:T(8,128)(2,1)}, bf16[288,1536]{1,0:T(8,128)(2,1)}, u32[]{:S(2)}, u32[]{:S(2)}) collective-permute-start(bf16[288,1536]{1,0:T(8,128)(2,1)} %get-tuple-element.120), channel_id=1, source_target_pairs={{0,8},{4,12},{8,0},{12,4},{16,24},{20,28},{24,16},{28,20},{1,9},{5... | collective-permute-start | bytes 2654216 | tf_op jit(solution)/shard_map/ppermute | solution.py:320
  267.0 31.7 %collective-permute-start.32 = (bf16[144,1152]{1,0:T(8,128)(2,1)}, bf16[144,1152]{1,0:T(8,128)(2,1)}, u32[]{:S(2)}, u32[]{:S(2)}) collective-permute-start(bf16[144,1152]{1,0:T(8,128)(2,1)} %get-tuple-element.134), channel_id=1, source_target_pairs={{0,4},{4,0},{8,12},{12,8},{16,20},{20,16},{24,28},{28,24},{1,5},{5... | collective-permute-start | bytes 995336 | tf_op jit(solution)/shard_map/ppermute | solution.py:320
  270.2 22.4 %collective-permute-start.47 = (bf16[96,1152]{1,0:T(8,128)(2,1)}, bf16[96,1152]{1,0:T(8,128)(2,1)S(1)}, u32[]{:S(2)}, u32[]{:S(2)}) collective-permute-start(bf16[96,1152]{1,0:T(8,128)(2,1)} %add_convert_fusion.15), channel_id=1, source_target_pairs={{0,4},{4,0},{8,12},{12,8},{16,20},{20,16},{24,28},{28,24},{1,5},{5... | collective-permute-start | bytes 663560 | tf_op jit(solution)/shard_map/ppermute | solution.py:320
  271.6 14.1 %collective-permute-start.21 = (bf16[256,1152]{1,0:T(8,128)(2,1)}, bf16[256,1152]{1,0:T(8,128)(2,1)S(1)}, u32[]{:S(2)}, u32[]{:S(2)}) collective-permute-start(bf16[256,1152]{1,0:T(8,128)(2,1)} %add_convert_fusion.7), channel_id=1, source_target_pairs={{0,2},{1,3},{2,0},{3,1},{4,6},{5,7},{6,4},{7,5},{8,10},{9,11},{10,... | collective-permute-start | bytes 1769480 | tf_op jit(solution)/shard_map/ppermute | solution.py:320
  291.1 16.7 %collective-permute-start.53 = (f32[1,7168]{1,0:T(1,128)}, f32[1,7168]{1,0:T(1,128)}, u32[]{:S(2)}, u32[]{:S(2)}) collective-permute-start(f32[1,7168]{1,0:T(1,128)} %constant_dynamic-update-slice_fusion.9), channel_id=1, source_target_pairs={{0,2},{1,3},{2,0},{3,1},{4,6},{5,7},{6,4},{7,5},{8,10},{9,11},{10,... | collective-permute-start | bytes 86024 | tf_op jit(solution)/shard_map/ppermute | solution.py:320
  293.4 53.1 %collective-permute-start.48 = (bf16[192,1152]{1,0:T(8,128)(2,1)}, bf16[192,1152]{1,0:T(8,128)(2,1)}, u32[]{:S(2)}, u32[]{:S(2)}) collective-permute-start(bf16[192,1152]{1,0:T(8,128)(2,1)} %maximum_select_fusion.12), channel_id=1, source_target_pairs={{0,16},{4,20},{8,24},{12,28},{16,0},{20,4},{24,8},{28,12},{1,17},{... | collective-permute-start | bytes 1327112 | tf_op jit(solution)/shard_map/ppermute | solution.py:320
  296.1 55.1 %collective-permute-start.40 = (bf16[144,1536]{1,0:T(8,128)(2,1)}, bf16[144,1536]{1,0:T(8,128)(2,1)}, u32[]{:S(2)}, u32[]{:S(2)}) collective-permute-start(bf16[144,1536]{1,0:T(8,128)(2,1)} %constant_dynamic-slice_fusion.6), channel_id=1, source_target_pairs={{0,16},{4,20},{8,24},{12,28},{16,0},{20,4},{24,8},{28,12},{1,17},{... | collective-permute-start | bytes 1327112 | tf_op jit(solution)/shard_map/ppermute | solution.py:320
  300.5 17.3 %collective-permute-start.33 = (bf16[72,1152]{1,0:T(8,128)(2,1)}, bf16[72,1152]{1,0:T(8,128)(2,1)}, u32[]{:S(2)}, u32[]{:S(2)}) collective-permute-start(bf16[72,1152]{1,0:T(8,128)(2,1)} %constant_dynamic-slice_fusion.12), channel_id=1, source_target_pairs={{0,8},{4,12},{8,0},{12,4},{16,24},{20,28},{24,16},{28,20},{1,9},{5... | collective-permute-start | bytes 497672 | tf_op jit(solution)/shard_map/ppermute | solution.py:320
  305.5 54.8 %collective-permute-start.27 = (bf16[288,864]{1,0:T(8,128)(2,1)}, bf16[288,864]{1,0:T(8,128)(2,1)}, u32[]{:S(2)}, u32[]{:S(2)}) collective-permute-start(bf16[288,864]{1,0:T(8,128)(2,1)} %copy.53), channel_id=1, source_target_pairs={{0,8},{4,12},{8,0},{12,4},{16,24},{20,28},{24,16},{28,20},{1,9},{5... | collective-permute-start | bytes 1493000 | tf_op jit(solution)/shard_map/ppermute | solution.py:320
  313.2 23.8 %collective-permute-start.55 = (bf16[4,7168]{1,0:T(4,128)(2,1)S(1)}, bf16[4,7168]{1,0:T(4,128)(2,1)S(1)}, u32[]{:S(2)}, u32[]{:S(2)}) collective-permute-start(bf16[4,7168]{1,0:T(4,128)(2,1)S(1)} %pad_maximum_fusion.8), channel_id=1, source_target_pairs={{0,16},{4,20},{8,24},{12,28},{16,0},{20,4},{24,8},{28,12},{1,17},{... | collective-permute-start | bytes 172040 | tf_op jit(solution)/shard_map/ppermute | solution.py:320
  318.8 20.1 %collective-permute-start.34 = (bf16[36,1152]{1,0:T(8,128)(2,1)S(1)}, bf16[36,1152]{1,0:T(8,128)(2,1)S(1)}, u32[]{:S(2)}, u32[]{:S(2)}) collective-permute-start(bf16[36,1152]{1,0:T(8,128)(2,1)S(1)} %constant_dynamic-slice_fusion.11), channel_id=1, source_target_pairs={{0,16},{4,20},{8,24},{12,28},{16,0},{20,4},{24,8},{28,12},{1,17},{... | collective-permute-start | bytes 248840 | tf_op jit(solution)/shard_map/ppermute | solution.py:320
  339.0 6.8 %collective-permute-start.35 = (bf16[36,1152]{1,0:T(8,128)(2,1)S(1)}, bf16[36,1152]{1,0:T(8,128)(2,1)S(1)}, u32[]{:S(2)}, u32[]{:S(2)}) collective-permute-start(bf16[36,1152]{1,0:T(8,128)(2,1)S(1)} %add_convert_fusion.17), channel_id=1, source_target_pairs={{0,16},{4,20},{8,24},{12,28},{16,0},{20,4},{24,8},{28,12},{1,17},{... | collective-permute-start | bytes 248840 | tf_op jit(solution)/shard_map/ppermute | solution.py:320
  342.2 10.9 %collective-permute-start.57 = (bf16[16,7168]{1,0:T(8,128)(2,1)S(1)}, bf16[16,7168]{1,0:T(8,128)(2,1)S(1)}, u32[]{:S(2)}, u32[]{:S(2)}) collective-permute-start(bf16[16,7168]{1,0:T(8,128)(2,1)S(1)} %pad_maximum_fusion.4), channel_id=1, source_target_pairs={{0,4},{4,0},{8,12},{12,8},{16,20},{20,16},{24,28},{28,24},{1,5},{5... | collective-permute-start | bytes 688136 | tf_op jit(solution)/shard_map/ppermute | solution.py:320
  346.5 53.1 %collective-permute-start.36 = (bf16[72,1152]{1,0:T(8,128)(2,1)}, bf16[72,1152]{1,0:T(8,128)(2,1)}, u32[]{:S(2)}, u32[]{:S(2)}) collective-permute-start(bf16[72,1152]{1,0:T(8,128)(2,1)} %maximum_select_fusion.14), channel_id=1, source_target_pairs={{0,8},{4,12},{8,0},{12,4},{16,24},{20,28},{24,16},{28,20},{1,9},{5... | collective-permute-start | bytes 497672 | tf_op jit(solution)/shard_map/ppermute | solution.py:320
  349.2 99.7 %collective-permute-start.49 = (bf16[384,1152]{1,0:T(8,128)(2,1)}, bf16[384,1152]{1,0:T(8,128)(2,1)}, u32[]{:S(2)}, u32[]{:S(2)}) collective-permute-start(bf16[384,1152]{1,0:T(8,128)(2,1)} %maximum_select_fusion.6), channel_id=1, source_target_pairs={{0,8},{4,12},{8,0},{12,4},{16,24},{20,28},{24,16},{28,20},{1,9},{5... | collective-permute-start | bytes 2654216 | tf_op jit(solution)/shard_map/ppermute | solution.py:320
  353.1 41.1 %collective-permute-start.41 = (bf16[144,1536]{1,0:T(8,128)(2,1)}, bf16[144,1536]{1,0:T(8,128)(2,1)}, u32[]{:S(2)}, u32[]{:S(2)}) collective-permute-start(bf16[144,1536]{1,0:T(8,128)(2,1)} %add_convert_fusion.12), channel_id=1, source_target_pairs={{0,16},{4,20},{8,24},{12,28},{16,0},{20,4},{24,8},{28,12},{1,17},{... | collective-permute-start | bytes 1327112 | tf_op jit(solution)/shard_map/ppermute | solution.py:320
  362.5 31.4 %collective-permute-start.28 = (bf16[144,864]{0,1:T(8,128)(2,1)S(1)}, bf16[144,864]{0,1:T(8,128)(2,1)S(1)}, u32[]{:S(2)}, u32[]{:S(2)}) collective-permute-start(bf16[144,864]{0,1:T(8,128)(2,1)S(1)} %constant_dynamic-slice_fusion.15), channel_id=1, source_target_pairs={{0,16},{4,20},{8,24},{12,28},{16,0},{20,4},{24,8},{28,12},{1,17},{... | collective-permute-start | bytes 746504 | tf_op jit(solution)/shard_map/ppermute | solution.py:320
  394.1 20.5 %collective-permute-start.29 = (bf16[144,864]{0,1:T(8,128)(2,1)S(1)}, bf16[144,864]{0,1:T(8,128)(2,1)S(1)}, u32[]{:S(2)}, u32[]{:S(2)}) collective-permute-start(bf16[144,864]{0,1:T(8,128)(2,1)S(1)} %add_convert_fusion.13), channel_id=1, source_target_pairs={{0,16},{4,20},{8,24},{12,28},{16,0},{20,4},{24,8},{28,12},{1,17},{... | collective-permute-start | bytes 746504 | tf_op jit(solution)/shard_map/ppermute | solution.py:320
  396.8 47.3 %collective-permute-start.42 = (bf16[288,1536]{1,0:T(8,128)(2,1)}, bf16[288,1536]{1,0:T(8,128)(2,1)}, u32[]{:S(2)}, u32[]{:S(2)}) collective-permute-start(bf16[288,1536]{1,0:T(8,128)(2,1)} %maximum_select_fusion.5), channel_id=1, source_target_pairs={{0,8},{4,12},{8,0},{12,4},{16,24},{20,28},{24,16},{28,20},{1,9},{5... | collective-permute-start | bytes 2654216 | tf_op jit(solution)/shard_map/ppermute | solution.py:320
  400.8 15.9 %collective-permute-start.37 = (bf16[144,1152]{1,0:T(8,128)(2,1)S(1)}, bf16[144,1152]{1,0:T(8,128)(2,1)}, u32[]{:S(2)}, u32[]{:S(2)}) collective-permute-start(bf16[144,1152]{1,0:T(8,128)(2,1)S(1)} %maximum_select_fusion.13), channel_id=1, source_target_pairs={{0,4},{4,0},{8,12},{12,8},{16,20},{20,16},{24,28},{28,24},{1,5},{5... | collective-permute-start | bytes 995336 | tf_op jit(solution)/shard_map/ppermute | solution.py:320
  416.2 21.8 %collective-permute-start.30 = (bf16[288,864]{1,0:T(8,128)(2,1)}, bf16[288,864]{1,0:T(8,128)(2,1)S(1)}, u32[]{:S(2)}, u32[]{:S(2)}) collective-permute-start(bf16[288,864]{1,0:T(8,128)(2,1)} %copy.55), channel_id=1, source_target_pairs={{0,8},{4,12},{8,0},{12,4},{16,24},{20,28},{24,16},{28,20},{1,9},{5... | collective-permute-start | bytes 1493000 | tf_op jit(solution)/shard_map/ppermute | solution.py:320
  443.3 26.0 %collective-permute-start.31 = (bf16[576,864]{1,0:T(8,128)(2,1)}, bf16[576,864]{1,0:T(8,128)(2,1)S(1)}, u32[]{:S(2)}, u32[]{:S(2)}) collective-permute-start(bf16[576,864]{1,0:T(8,128)(2,1)} %copy.58), channel_id=1, source_target_pairs={{0,4},{4,0},{8,12},{12,8},{16,20},{20,16},{24,28},{28,24},{1,5},{5... | collective-permute-start | bytes 2985992 | tf_op jit(solution)/shard_map/ppermute | solution.py:320
  447.7 55.9 %collective-permute-start.43 = (bf16[576,1536]{1,0:T(8,128)(2,1)}, bf16[576,1536]{1,0:T(8,128)(2,1)}, u32[]{:S(2)}, u32[]{:S(2)}) collective-permute-start(bf16[576,1536]{1,0:T(8,128)(2,1)} %maximum_select_fusion), channel_id=1, source_target_pairs={{0,4},{4,0},{8,12},{12,8},{16,20},{20,16},{24,28},{28,24},{1,5},{5... | collective-permute-start | bytes 5308424 | tf_op jit(solution)/shard_map/ppermute | solution.py:320
  (97 other events, 649.3 us)
